TPU v7x, 512 devices: a whole 4x8x8 slice. The times are simulated.
512 devices in a mesh: seq: 32 (over x, z), exp: 16 (over y, core).
Axes of the slice: x: 4, y: 8, z: 8, core: 2. Of those that a mesh axis runs over, the one named last changes fastest.
Arguments:
- queries: bfloat16 [8192, 2048], P('seq', 'exp'), may hold values from -112 to 112
- key_rows: bfloat16 [8192, 2048], P('seq', 'exp'), may hold values from -4 to 4
- value_rows: bfloat16 [8192, 2048], P('seq', 'exp'), may hold values from -6 to 6
- out_grad: bfloat16 [8192, 2048], P('seq', 'exp'), may hold values from -6 to 6
- expert_ids: int32 [8192, 2], P('seq'), may hold values from 0 to 31, all different within a row
- gate_values: float32 [8192, 2], P('seq'), may hold values from 0.1 to 1
- alibi_slope: float32 [16], P('exp'), may hold values from 0.00012207031 to 0.1
- expert_in: bfloat16 [32, 2048, 4096], P('seq', None, 'exp'), may hold values from -0.125 to 0.125
- expert_out: bfloat16 [32, 4096, 2048], P('seq', 'exp'), may hold values from -0.09375 to 0.09375
Outputs:
- query_grad: bfloat16 [8192, 2048], P('seq', 'exp')
- key_grad: bfloat16 [8192, 2048], P('seq', 'exp')
- value_grad: bfloat16 [8192, 2048], P('seq', 'exp')
- expert_in_grad: bfloat16 [32, 2048, 4096], P('seq', None, 'exp')
- expert_out_grad: bfloat16 [32, 4096, 2048], P('seq', 'exp')
Inputs may be any that keep to these rules, and one draw needn't show every extreme that they name: `expert_ids`: each token names two different experts.
All inputs are finite; a program needn't handle non-finite values.
Results may differ from a plain program's by a relative error of at most 0.024.
Values may be sent and summed in bfloat16 or wider, within the bound.
A program may use at most 128 MiB of HBM per device.

v0:
```python
import jax
import jax.numpy as jnp
from jax import lax
from jax.sharding import PartitionSpec as P

HD = 128
WCH = 16


def shifted(block, axis, distance):
    devices = range(lax.axis_size(axis))
    route = [(i - distance, i) for i in devices if i - distance in devices]
    return lax.ppermute(block, axis, route)


def window_scores(query_heads, key_stack, slopes, seq_index, window):
    score_scale = HD ** (-0.5)
    block_len = query_heads.shape[0]
    raw_scores = (
        jnp.einsum("ihd,jhd->hij", query_heads, key_stack, preferred_element_type=jnp.float32)
        * score_scale
    )
    row_pos = lax.broadcasted_iota(jnp.int32, (block_len, key_stack.shape[0]), 0)
    col_pos = lax.broadcasted_iota(jnp.int32, (block_len, key_stack.shape[0]), 1)
    back_block = col_pos // block_len
    distance = row_pos - col_pos % block_len + back_block * block_len
    in_window = (distance >= 0) & (distance < window) & (seq_index - back_block >= 0)
    biased = raw_scores - slopes[:, None, None] * distance.astype(jnp.float32)[None]
    return jnp.where(in_window[None], biased, -jnp.inf)


def slot_routing(expert_ids, experts, capacity):
    flat_ids = jnp.concatenate([expert_ids[:, 0], expert_ids[:, 1]])
    entry_count = flat_ids.shape[0]
    expert_cols = lax.broadcasted_iota(jnp.int32, (entry_count, experts), 1)
    one_hot = (flat_ids[:, None] == expert_cols).astype(jnp.int32)
    before = jnp.cumsum(one_hot, axis=0) - one_hot
    position = jnp.sum(before * one_hot, axis=1)
    is_kept = position < capacity
    slot_index = flat_ids * capacity + position
    slot_rows = lax.broadcasted_iota(jnp.int32, (experts * capacity, entry_count), 0)
    return ((slot_rows == slot_index[None, :]) & is_kept[None, :]).astype(jnp.bfloat16)


def per_device(
    queries,
    key_rows,
    value_rows,
    out_grad,
    expert_ids,
    gate_values,
    alibi_slope,
    expert_in,
    expert_out,
):
    score_scale = HD ** (-0.5)
    block_len = queries.shape[0]
    features = queries.shape[1]
    head_count = features // HD
    seq_index = lax.axis_index("seq")
    stretches = WCH + 1
    window = WCH * block_len

    def relay_keys(step, carry):
        stack_keys, stack_values, current_keys, current_values = carry
        current_keys, current_values = shifted((current_keys, current_values), "seq", 1)
        stack_keys = lax.dynamic_update_index_in_dim(stack_keys, current_keys, step, 0)
        stack_values = lax.dynamic_update_index_in_dim(stack_values, current_values, step, 0)
        return (stack_keys, stack_values, current_keys, current_values)

    empty_stack = jnp.zeros((stretches, block_len, features), jnp.bfloat16)
    start_keys = lax.dynamic_update_index_in_dim(empty_stack, key_rows, 0, 0)
    start_values = lax.dynamic_update_index_in_dim(empty_stack, value_rows, 0, 0)
    key_stack, value_stack, unused_keys, unused_values = lax.fori_loop(
        1, stretches, relay_keys, (start_keys, start_values, key_rows, value_rows)
    )
    key_block = key_stack.reshape(stretches * block_len, head_count, HD)
    value_block = value_stack.reshape(stretches * block_len, head_count, HD)
    query_heads = queries.reshape(block_len, head_count, HD)
    scores = window_scores(query_heads, key_block, alibi_slope, seq_index, window)
    log_norm = jax.nn.logsumexp(scores, axis=2)
    probs_full = jnp.exp(scores - log_norm[:, :, None])
    weights = probs_full.astype(jnp.bfloat16)
    attn_heads = jnp.einsum(
        "hij,jhd->ihd", weights, value_block, preferred_element_type=jnp.float32
    ).astype(jnp.bfloat16)
    attn_out = attn_heads.reshape(block_len, features)
    experts = lax.axis_size("seq")
    capacity = 5 * block_len // (2 * experts)
    routing = slot_routing(expert_ids, experts, capacity)
    both_tokens = jnp.concatenate([attn_out, attn_out])
    scaled_grad = jnp.concatenate(
        [gate_values[:, 0:1] * out_grad, gate_values[:, 1:2] * out_grad]
    ).astype(jnp.bfloat16)
    send_tokens = jnp.dot(routing, both_tokens, preferred_element_type=jnp.float32).astype(
        jnp.bfloat16
    )
    send_grads = jnp.dot(routing, scaled_grad, preferred_element_type=jnp.float32).astype(
        jnp.bfloat16
    )
    recv_tokens, recv_grads = (
        lax.all_to_all(send_tokens, "seq", split_axis=0, concat_axis=0, tiled=True),
        lax.all_to_all(send_grads, "seq", split_axis=0, concat_axis=0, tiled=True),
    )
    weight_in = expert_in[0]
    weight_out = expert_out[0]
    full_tokens = lax.all_gather(recv_tokens, "exp", axis=1, tiled=True)
    pre_act = jnp.dot(full_tokens, weight_in, preferred_element_type=jnp.float32)
    full_grads = lax.all_gather(recv_grads, "exp", axis=1, tiled=True)
    logistic = jax.nn.sigmoid(pre_act)
    hidden = (pre_act * logistic).astype(jnp.bfloat16)
    through_out = lax.dot_general(
        full_grads, weight_out, (((1,), (1,)), ((), ())), preferred_element_type=jnp.float32
    )
    hidden_grad = (through_out * logistic * (1.0 + pre_act * (1.0 - logistic))).astype(jnp.bfloat16)
    out_weight_grad = lax.dot_general(
        hidden, full_grads, (((0,), (0,)), ((), ())), preferred_element_type=jnp.float32
    ).astype(jnp.bfloat16)
    in_weight_grad = lax.dot_general(
        full_tokens, hidden_grad, (((0,), (0,)), ((), ())), preferred_element_type=jnp.float32
    ).astype(jnp.bfloat16)
    back_rows = lax.psum_scatter(
        lax.dot_general(
            weight_in, hidden_grad, (((1,), (1,)), ((), ())), preferred_element_type=jnp.float32
        ).astype(jnp.bfloat16),
        "exp",
        scatter_dimension=0,
        tiled=True,
    )
    returned = lax.all_to_all(back_rows, "seq", split_axis=1, concat_axis=1, tiled=True)
    combined = lax.dot_general(
        routing, returned, (((0,), (1,)), ((), ())), preferred_element_type=jnp.float32
    )
    attn_grad = (out_grad.astype(jnp.float32) + combined[:block_len] + combined[block_len:]).astype(
        jnp.bfloat16
    )
    grad_heads = attn_grad.reshape(block_len, head_count, HD)
    row_delta = jnp.einsum(
        "ihd,ihd->hi", grad_heads, attn_heads, preferred_element_type=jnp.float32
    )
    dprob = jnp.einsum("ihd,jhd->hij", grad_heads, value_block, preferred_element_type=jnp.float32)
    dscore = (probs_full * (dprob - row_delta[:, :, None])).astype(jnp.bfloat16)
    query_grad = (
        jnp.einsum("hij,jhd->ihd", dscore, key_block, preferred_element_type=jnp.float32)
        * score_scale
    ).astype(jnp.bfloat16)
    key_parts = (
        jnp.einsum("hij,ihd->jhd", dscore, query_heads, preferred_element_type=jnp.float32)
        * score_scale
    ).reshape(stretches, block_len, features)
    value_parts = jnp.einsum(
        "hij,ihd->jhd", weights, grad_heads, preferred_element_type=jnp.float32
    ).reshape(stretches, block_len, features)

    def relay_grads(step, carry):
        key_acc, value_acc = carry
        key_acc, value_acc = (
            shifted(key_acc.astype(jnp.bfloat16), "seq", -1).astype(key_acc.dtype),
            shifted(value_acc.astype(jnp.bfloat16), "seq", -1).astype(value_acc.dtype),
        )
        index = stretches - 1 - step
        key_acc = key_acc + lax.dynamic_index_in_dim(key_parts, index, 0, keepdims=False)
        value_acc = value_acc + lax.dynamic_index_in_dim(value_parts, index, 0, keepdims=False)
        return (key_acc, value_acc)

    key_total, value_total = lax.fori_loop(
        1, stretches, relay_grads, (key_parts[stretches - 1], value_parts[stretches - 1])
    )
    key_grad = key_total.astype(jnp.bfloat16)
    value_grad = value_total.astype(jnp.bfloat16)
    return (
        query_grad.reshape(block_len, features),
        key_grad,
        value_grad,
        in_weight_grad[None],
        out_weight_grad[None],
    )


def solution(mesh):
    return jax.shard_map(
        per_device,
        mesh=mesh,
        in_specs=(
            P("seq", "exp"),
            P("seq", "exp"),
            P("seq", "exp"),
            P("seq", "exp"),
            P("seq", None),
            P("seq", None),
            P("exp"),
            P("seq", None, "exp"),
            P("seq", "exp", None),
        ),
        out_specs=(
            P("seq", "exp"),
            P("seq", "exp"),
            P("seq", "exp"),
            P("seq", None, "exp"),
            P("seq", "exp", None),
        ),
        check_vma=False,
    )
```

profile of v0, /device:TPU:6, one launch (start us, length us, event | category | flops | bytes accessed | tf_op | source)
XLA Modules:
  0.0 585.3 jit_solution(2084339012505833438)
XLA Ops:
  14.8 170.4 %while.36 = (s32[]{:T(128)}, bf16[17,256,128]{2,1,0:T(8,128)(2,1)S(1)}, bf16[17,256,128]{2,1,0:T(8,128)(2,1)S(1)}, bf16[256,128]{1,0:T(8,128)(2,1)S(1)}, bf16[25...) while((s32[]{:T(128)}, bf16[17,256,128]{2,1,0:T(8,128)(2,1)S(1)}, ...), condition=%wide.region_1.2_spmd, body=%wide.region_0.1_spmd.sunk | while | flops 5 | bytes 1048783 | solution.py:74
  14.8 4.3 collective-permute-start.1
  19.1 4.3 collective-permute-start
  23.4 4.9 collective-permute-done.1
  35.1 4.0 collective-permute-done.1
  42.4 3.5 collective-permute-start
  45.9 3.2 collective-permute-done.1
  52.7 3.7 collective-permute-start
  62.9 3.4 collective-permute-start
  76.2 3.4 collective-permute-done.1
  85.4 4.4 collective-permute-done.1
  95.6 4.4 collective-permute-done.1
  106.5 5.0 collective-permute-done.1
  117.3 4.4 collective-permute-done.1
  127.6 5.0 collective-permute-done.1
  137.8 4.8 collective-permute-done.1
  148.1 4.4 collective-permute-done.1
  158.3 4.4 collective-permute-done.1
  168.6 4.4 collective-permute-done.1
  178.8 4.4 collective-permute-done.1
  185.2 5.8 fusion.71
  195.0 14.9 %all_to_all.36 = bf16[32,20,128]{2,1,0:T(8,128)(2,1)} all-to-all(bf16[32,20,128]{2,1,0:T(8,128)(2,1)S(1)} %all_to_all.27), channel_id=1, replica_groups=mesh['seq'=32,'exp'=16] {'seq'}, dimensions={0} | all-to-all | bytes 327680 | tf_op jit(solution)/shard_map/all_to_all | solution.py:102
  214.6 15.9 %all_to_all.37 = bf16[32,20,128]{2,1,0:T(8,128)(2,1)} all-to-all(bf16[32,20,128]{2,1,0:T(8,128)(2,1)S(1)} %all_to_all.24), channel_id=1, replica_groups=mesh['seq'=32,'exp'=16] {'seq'}, dimensions={0} | all-to-all | bytes 327680 | tf_op jit(solution)/shard_map/all_to_all | solution.py:103
  232.2 23.5 %all-gather.5.cloned.1.call-done = bf16[640,2048]{1,0:T(8,128)(2,1)} async-done(((bf16[640,128]{1,0:T(8,128)(2,1)}), bf16[640,2048]{1,0:T(8,128)(2,1)}) %all-gather.5.cloned.1.call-update) | async-done | bytes 2621456 | tf_op jit(solution)/shard_map/all_gather | solution.py:107
  255.7 3.4 fusion.34
  259.1 43.8 %all-gather.3.cloned.1.call-done = bf16[640,2048]{1,0:T(8,128)(2,1)} async-done(((bf16[640,128]{1,0:T(8,128)(2,1)}), bf16[640,2048]{1,0:T(8,128)(2,1)}) %all-gather.3.cloned.1.call-update) | async-done | bytes 2621456 | tf_op jit(solution)/shard_map/all_gather | solution.py:109
  302.9 3.1 fusion.23
  309.2 4.4 copy.33
  313.6 4.0 fusion.14
  317.5 57.6 %reduce-scatter.4.cloned.1.call-done = bf16[128,640]{1,0:T(8,128)(2,1)} async-done(((bf16[2048,640]{1,0:T(8,128)(2,1)}), bf16[128,640]{1,0:T(8,128)(2,1)}) %reduce-scatter.4.cloned.1.call-update) | async-done | bytes 163856
  377.0 10.5 %all-to-all-start.2 = ((bf16[128,32,20]{0,2,1:T(8,128)(2,1)}), bf16[128,32,20]{0,2,1:T(8,128)(2,1)S(1)}, u32[]{:S(2)}, u32[]{:S(2)}) async-start(bf16[128,32,20]{0,2,1:T(8,128)(2,1)} %all_to_all.30), calls=%async_computation.2 | async-start | bytes 393216 | tf_op jit(solution)/shard_map/all_to_all | solution.py:130
  387.5 3.8 fusion.13
  391.3 5.0 all-to-all-done.2
  399.4 3.2 convolution_bitcast_fusion
  402.7 4.0 fusion.4
  412.1 165.9 %while.37 = (s32[]{:T(128)}, bf16[256,128]{1,0:T(8,128)(2,1)S(1)}, bf16[256,128]{1,0:T(8,128)(2,1)S(1)}, f32[17,256,128]{2,1,0:T(8,128)S(1)}, f32[17,256,128]{2,...) while((s32[]{:T(128)}, bf16[256,128]{1,0:T(8,128)(2,1)S(1)}, ...), condition=%wide.region_9.10_spmd, body=%wide.region_8.9_spmd.sunk | while | flops 196614 | bytes 1048803 | solution.py:166
  415.2 3.1 collective-permute-start.2
  421.7 4.8 collective-permute-start.3
  429.4 3.3 collective-permute-done.2
  432.8 4.2 collective-permute-start.3
  439.9 3.3 collective-permute-done.2
  443.2 4.0 collective-permute-start.3
  450.7 3.1 collective-permute-done.2
  453.8 4.3 collective-permute-start.3
  461.0 3.3 collective-permute-done.2
  464.4 4.0 collective-permute-start.3
  474.6 4.0 collective-permute-start.3
  481.7 3.1 collective-permute-done.2
  484.8 4.0 collective-permute-start.3
  491.9 3.1 collective-permute-done.2
  495.0 4.0 collective-permute-start.3
  505.3 4.0 collective-permute-start.3
  512.4 3.6 collective-permute-done.2
  516.0 3.6 collective-permute-start.3
  525.7 4.0 collective-permute-start.3
  532.8 3.1 collective-permute-done.2
  536.0 4.6 collective-permute-start.3
  543.9 3.4 collective-permute-done.2
  547.3 4.2 collective-permute-start.3
  554.3 3.2 collective-permute-done.2
  557.6 4.0 collective-permute-start.3
  564.7 3.1 collective-permute-done.2
  567.8 4.0 collective-permute-start.3
  574.9 3.1 collective-permute-done.2
  (248 shorter events, 182.5 us)
Async XLA Ops:
  7.2 248.5 %all-gather.5.cloned.1.call-start = ((), (), s32[]{:S(2)}) async-start(), calls=%async_computation.5 | async-start | bytes 2785280 | tf_op jit(solution)/shard_map/all_gather | solution.py:107
  14.8 13.5 %collective-permute-start.1 = (bf16[256,128]{1,0:T(8,128)(2,1)S(1)}, bf16[256,128]{1,0:T(8,128)(2,1)S(1)}, u32[]{:S(2)}, u32[]{:S(2)}) collective-permute-start(bf16[256,128]{1,0:T(8,128)(2,1)S(1)} %get-tuple-element.375), channel_id=1, source_target_pairs={{0,16},{16,32},{32,48},{48,64},{64,80},{80,96},{96,112},{112,128},... | collective-permute-start | bytes 196616 | tf_op jit(solution)/shard_map/while/body/eval_jaxpr/ppermute | solution.py:13
  19.1 11.1 %collective-permute-start = (bf16[256,128]{1,0:T(8,128)(2,1)S(1)}, bf16[256,128]{1,0:T(8,128)(2,1)S(1)}, u32[]{:S(2)}, u32[]{:S(2)}) collective-permute-start(bf16[256,128]{1,0:T(8,128)(2,1)S(1)} %get-tuple-element.374), channel_id=1, source_target_pairs={{0,16},{16,32},{32,48},{48,64},{64,80},{80,96},{96,112},{112,128},... | collective-permute-start | bytes 196616 | tf_op jit(solution)/shard_map/while/body/eval_jaxpr/ppermute | solution.py:13
  30.3 8.9 %collective-permute-start.1 = (bf16[256,128]{1,0:T(8,128)(2,1)S(1)}, bf16[256,128]{1,0:T(8,128)(2,1)S(1)}, u32[]{:S(2)}, u32[]{:S(2)}) collective-permute-start(bf16[256,128]{1,0:T(8,128)(2,1)S(1)} %get-tuple-element.375), channel_id=1, source_target_pairs={{0,16},{16,32},{32,48},{48,64},{64,80},{80,96},{96,112},{112,128},... | collective-permute-start | bytes 196616 | tf_op jit(solution)/shard_map/while/body/eval_jaxpr/ppermute | solution.py:13
  32.2 8.3 %collective-permute-start = (bf16[256,128]{1,0:T(8,128)(2,1)S(1)}, bf16[256,128]{1,0:T(8,128)(2,1)S(1)}, u32[]{:S(2)}, u32[]{:S(2)}) collective-permute-start(bf16[256,128]{1,0:T(8,128)(2,1)S(1)} %get-tuple-element.374), channel_id=1, source_target_pairs={{0,16},{16,32},{32,48},{48,64},{64,80},{80,96},{96,112},{112,128},... | collective-permute-start | bytes 196616 | tf_op jit(solution)/shard_map/while/body/eval_jaxpr/ppermute | solution.py:13
  40.5 8.7 %collective-permute-start.1 = (bf16[256,128]{1,0:T(8,128)(2,1)S(1)}, bf16[256,128]{1,0:T(8,128)(2,1)S(1)}, u32[]{:S(2)}, u32[]{:S(2)}) collective-permute-start(bf16[256,128]{1,0:T(8,128)(2,1)S(1)} %get-tuple-element.375), channel_id=1, source_target_pairs={{0,16},{16,32},{32,48},{48,64},{64,80},{80,96},{96,112},{112,128},... | collective-permute-start | bytes 196616 | tf_op jit(solution)/shard_map/while/body/eval_jaxpr/ppermute | solution.py:13
  42.4 8.3 %collective-permute-start = (bf16[256,128]{1,0:T(8,128)(2,1)S(1)}, bf16[256,128]{1,0:T(8,128)(2,1)S(1)}, u32[]{:S(2)}, u32[]{:S(2)}) collective-permute-start(bf16[256,128]{1,0:T(8,128)(2,1)S(1)} %get-tuple-element.374), channel_id=1, source_target_pairs={{0,16},{16,32},{32,48},{48,64},{64,80},{80,96},{96,112},{112,128},... | collective-permute-start | bytes 196616 | tf_op jit(solution)/shard_map/while/body/eval_jaxpr/ppermute | solution.py:13
  50.8 8.3 %collective-permute-start.1 = (bf16[256,128]{1,0:T(8,128)(2,1)S(1)}, bf16[256,128]{1,0:T(8,128)(2,1)S(1)}, u32[]{:S(2)}, u32[]{:S(2)}) collective-permute-start(bf16[256,128]{1,0:T(8,128)(2,1)S(1)} %get-tuple-element.375), channel_id=1, source_target_pairs={{0,16},{16,32},{32,48},{48,64},{64,80},{80,96},{96,112},{112,128},... | collective-permute-start | bytes 196616 | tf_op jit(solution)/shard_map/while/body/eval_jaxpr/ppermute | solution.py:13
  52.7 8.3 %collective-permute-start = (bf16[256,128]{1,0:T(8,128)(2,1)S(1)}, bf16[256,128]{1,0:T(8,128)(2,1)S(1)}, u32[]{:S(2)}, u32[]{:S(2)}) collective-permute-start(bf16[256,128]{1,0:T(8,128)(2,1)S(1)} %get-tuple-element.374), channel_id=1, source_target_pairs={{0,16},{16,32},{32,48},{48,64},{64,80},{80,96},{96,112},{112,128},... | collective-permute-start | bytes 196616 | tf_op jit(solution)/shard_map/while/body/eval_jaxpr/ppermute | solution.py:13
  61.0 8.3 %collective-permute-start.1 = (bf16[256,128]{1,0:T(8,128)(2,1)S(1)}, bf16[256,128]{1,0:T(8,128)(2,1)S(1)}, u32[]{:S(2)}, u32[]{:S(2)}) collective-permute-start(bf16[256,128]{1,0:T(8,128)(2,1)S(1)} %get-tuple-element.375), channel_id=1, source_target_pairs={{0,16},{16,32},{32,48},{48,64},{64,80},{80,96},{96,112},{112,128},... | collective-permute-start | bytes 196616 | tf_op jit(solution)/shard_map/while/body/eval_jaxpr/ppermute | solution.py:13
  62.9 8.3 %collective-permute-start = (bf16[256,128]{1,0:T(8,128)(2,1)S(1)}, bf16[256,128]{1,0:T(8,128)(2,1)S(1)}, u32[]{:S(2)}, u32[]{:S(2)}) collective-permute-start(bf16[256,128]{1,0:T(8,128)(2,1)S(1)} %get-tuple-element.374), channel_id=1, source_target_pairs={{0,16},{16,32},{32,48},{48,64},{64,80},{80,96},{96,112},{112,128},... | collective-permute-start | bytes 196616 | tf_op jit(solution)/shard_map/while/body/eval_jaxpr/ppermute | solution.py:13
  71.3 8.3 %collective-permute-start.1 = (bf16[256,128]{1,0:T(8,128)(2,1)S(1)}, bf16[256,128]{1,0:T(8,128)(2,1)S(1)}, u32[]{:S(2)}, u32[]{:S(2)}) collective-permute-start(bf16[256,128]{1,0:T(8,128)(2,1)S(1)} %get-tuple-element.375), channel_id=1, source_target_pairs={{0,16},{16,32},{32,48},{48,64},{64,80},{80,96},{96,112},{112,128},... | collective-permute-start | bytes 196616 | tf_op jit(solution)/shard_map/while/body/eval_jaxpr/ppermute | solution.py:13
  73.2 8.3 %collective-permute-start = (bf16[256,128]{1,0:T(8,128)(2,1)S(1)}, bf16[256,128]{1,0:T(8,128)(2,1)S(1)}, u32[]{:S(2)}, u32[]{:S(2)}) collective-permute-start(bf16[256,128]{1,0:T(8,128)(2,1)S(1)} %get-tuple-element.374), channel_id=1, source_target_pairs={{0,16},{16,32},{32,48},{48,64},{64,80},{80,96},{96,112},{112,128},... | collective-permute-start | bytes 196616 | tf_op jit(solution)/shard_map/while/body/eval_jaxpr/ppermute | solution.py:13
  81.5 8.3 %collective-permute-start.1 = (bf16[256,128]{1,0:T(8,128)(2,1)S(1)}, bf16[256,128]{1,0:T(8,128)(2,1)S(1)}, u32[]{:S(2)}, u32[]{:S(2)}) collective-permute-start(bf16[256,128]{1,0:T(8,128)(2,1)S(1)} %get-tuple-element.375), channel_id=1, source_target_pairs={{0,16},{16,32},{32,48},{48,64},{64,80},{80,96},{96,112},{112,128},... | collective-permute-start | bytes 196616 | tf_op jit(solution)/shard_map/while/body/eval_jaxpr/ppermute | solution.py:13
  83.4 8.3 %collective-permute-start = (bf16[256,128]{1,0:T(8,128)(2,1)S(1)}, bf16[256,128]{1,0:T(8,128)(2,1)S(1)}, u32[]{:S(2)}, u32[]{:S(2)}) collective-permute-start(bf16[256,128]{1,0:T(8,128)(2,1)S(1)} %get-tuple-element.374), channel_id=1, source_target_pairs={{0,16},{16,32},{32,48},{48,64},{64,80},{80,96},{96,112},{112,128},... | collective-permute-start | bytes 196616 | tf_op jit(solution)/shard_map/while/body/eval_jaxpr/ppermute | solution.py:13
  91.8 8.3 %collective-permute-start.1 = (bf16[256,128]{1,0:T(8,128)(2,1)S(1)}, bf16[256,128]{1,0:T(8,128)(2,1)S(1)}, u32[]{:S(2)}, u32[]{:S(2)}) collective-permute-start(bf16[256,128]{1,0:T(8,128)(2,1)S(1)} %get-tuple-element.375), channel_id=1, source_target_pairs={{0,16},{16,32},{32,48},{48,64},{64,80},{80,96},{96,112},{112,128},... | collective-permute-start | bytes 196616 | tf_op jit(solution)/shard_map/while/body/eval_jaxpr/ppermute | solution.py:13
  93.7 8.9 %collective-permute-start = (bf16[256,128]{1,0:T(8,128)(2,1)S(1)}, bf16[256,128]{1,0:T(8,128)(2,1)S(1)}, u32[]{:S(2)}, u32[]{:S(2)}) collective-permute-start(bf16[256,128]{1,0:T(8,128)(2,1)S(1)} %get-tuple-element.374), channel_id=1, source_target_pairs={{0,16},{16,32},{32,48},{48,64},{64,80},{80,96},{96,112},{112,128},... | collective-permute-start | bytes 196616 | tf_op jit(solution)/shard_map/while/body/eval_jaxpr/ppermute | solution.py:13
  102.6 8.9 %collective-permute-start.1 = (bf16[256,128]{1,0:T(8,128)(2,1)S(1)}, bf16[256,128]{1,0:T(8,128)(2,1)S(1)}, u32[]{:S(2)}, u32[]{:S(2)}) collective-permute-start(bf16[256,128]{1,0:T(8,128)(2,1)S(1)} %get-tuple-element.375), channel_id=1, source_target_pairs={{0,16},{16,32},{32,48},{48,64},{64,80},{80,96},{96,112},{112,128},... | collective-permute-start | bytes 196616 | tf_op jit(solution)/shard_map/while/body/eval_jaxpr/ppermute | solution.py:13
  104.5 8.9 %collective-permute-start = (bf16[256,128]{1,0:T(8,128)(2,1)S(1)}, bf16[256,128]{1,0:T(8,128)(2,1)S(1)}, u32[]{:S(2)}, u32[]{:S(2)}) collective-permute-start(bf16[256,128]{1,0:T(8,128)(2,1)S(1)} %get-tuple-element.374), channel_id=1, source_target_pairs={{0,16},{16,32},{32,48},{48,64},{64,80},{80,96},{96,112},{112,128},... | collective-permute-start | bytes 196616 | tf_op jit(solution)/shard_map/while/body/eval_jaxpr/ppermute | solution.py:13
  113.5 8.3 %collective-permute-start.1 = (bf16[256,128]{1,0:T(8,128)(2,1)S(1)}, bf16[256,128]{1,0:T(8,128)(2,1)S(1)}, u32[]{:S(2)}, u32[]{:S(2)}) collective-permute-start(bf16[256,128]{1,0:T(8,128)(2,1)S(1)} %get-tuple-element.375), channel_id=1, source_target_pairs={{0,16},{16,32},{32,48},{48,64},{64,80},{80,96},{96,112},{112,128},... | collective-permute-start | bytes 196616 | tf_op jit(solution)/shard_map/while/body/eval_jaxpr/ppermute | solution.py:13
  115.4 8.3 %collective-permute-start = (bf16[256,128]{1,0:T(8,128)(2,1)S(1)}, bf16[256,128]{1,0:T(8,128)(2,1)S(1)}, u32[]{:S(2)}, u32[]{:S(2)}) collective-permute-start(bf16[256,128]{1,0:T(8,128)(2,1)S(1)} %get-tuple-element.374), channel_id=1, source_target_pairs={{0,16},{16,32},{32,48},{48,64},{64,80},{80,96},{96,112},{112,128},... | collective-permute-start | bytes 196616 | tf_op jit(solution)/shard_map/while/body/eval_jaxpr/ppermute | solution.py:13
  123.7 8.9 %collective-permute-start.1 = (bf16[256,128]{1,0:T(8,128)(2,1)S(1)}, bf16[256,128]{1,0:T(8,128)(2,1)S(1)}, u32[]{:S(2)}, u32[]{:S(2)}) collective-permute-start(bf16[256,128]{1,0:T(8,128)(2,1)S(1)} %get-tuple-element.375), channel_id=1, source_target_pairs={{0,16},{16,32},{32,48},{48,64},{64,80},{80,96},{96,112},{112,128},... | collective-permute-start | bytes 196616 | tf_op jit(solution)/shard_map/while/body/eval_jaxpr/ppermute | solution.py:13
  125.6 8.3 %collective-permute-start = (bf16[256,128]{1,0:T(8,128)(2,1)S(1)}, bf16[256,128]{1,0:T(8,128)(2,1)S(1)}, u32[]{:S(2)}, u32[]{:S(2)}) collective-permute-start(bf16[256,128]{1,0:T(8,128)(2,1)S(1)} %get-tuple-element.374), channel_id=1, source_target_pairs={{0,16},{16,32},{32,48},{48,64},{64,80},{80,96},{96,112},{112,128},... | collective-permute-start | bytes 196616 | tf_op jit(solution)/shard_map/while/body/eval_jaxpr/ppermute | solution.py:13
  134.0 8.7 %collective-permute-start.1 = (bf16[256,128]{1,0:T(8,128)(2,1)S(1)}, bf16[256,128]{1,0:T(8,128)(2,1)S(1)}, u32[]{:S(2)}, u32[]{:S(2)}) collective-permute-start(bf16[256,128]{1,0:T(8,128)(2,1)S(1)} %get-tuple-element.375), channel_id=1, source_target_pairs={{0,16},{16,32},{32,48},{48,64},{64,80},{80,96},{96,112},{112,128},... | collective-permute-start | bytes 196616 | tf_op jit(solution)/shard_map/while/body/eval_jaxpr/ppermute | solution.py:13
  135.9 8.3 %collective-permute-start = (bf16[256,128]{1,0:T(8,128)(2,1)S(1)}, bf16[256,128]{1,0:T(8,128)(2,1)S(1)}, u32[]{:S(2)}, u32[]{:S(2)}) collective-permute-start(bf16[256,128]{1,0:T(8,128)(2,1)S(1)} %get-tuple-element.374), channel_id=1, source_target_pairs={{0,16},{16,32},{32,48},{48,64},{64,80},{80,96},{96,112},{112,128},... | collective-permute-start | bytes 196616 | tf_op jit(solution)/shard_map/while/body/eval_jaxpr/ppermute | solution.py:13
  144.2 8.3 %collective-permute-start.1 = (bf16[256,128]{1,0:T(8,128)(2,1)S(1)}, bf16[256,128]{1,0:T(8,128)(2,1)S(1)}, u32[]{:S(2)}, u32[]{:S(2)}) collective-permute-start(bf16[256,128]{1,0:T(8,128)(2,1)S(1)} %get-tuple-element.375), channel_id=1, source_target_pairs={{0,16},{16,32},{32,48},{48,64},{64,80},{80,96},{96,112},{112,128},... | collective-permute-start | bytes 196616 | tf_op jit(solution)/shard_map/while/body/eval_jaxpr/ppermute | solution.py:13
  146.1 8.3 %collective-permute-start = (bf16[256,128]{1,0:T(8,128)(2,1)S(1)}, bf16[256,128]{1,0:T(8,128)(2,1)S(1)}, u32[]{:S(2)}, u32[]{:S(2)}) collective-permute-start(bf16[256,128]{1,0:T(8,128)(2,1)S(1)} %get-tuple-element.374), channel_id=1, source_target_pairs={{0,16},{16,32},{32,48},{48,64},{64,80},{80,96},{96,112},{112,128},... | collective-permute-start | bytes 196616 | tf_op jit(solution)/shard_map/while/body/eval_jaxpr/ppermute | solution.py:13
  154.5 8.3 %collective-permute-start.1 = (bf16[256,128]{1,0:T(8,128)(2,1)S(1)}, bf16[256,128]{1,0:T(8,128)(2,1)S(1)}, u32[]{:S(2)}, u32[]{:S(2)}) collective-permute-start(bf16[256,128]{1,0:T(8,128)(2,1)S(1)} %get-tuple-element.375), channel_id=1, source_target_pairs={{0,16},{16,32},{32,48},{48,64},{64,80},{80,96},{96,112},{112,128},... | collective-permute-start | bytes 196616 | tf_op jit(solution)/shard_map/while/body/eval_jaxpr/ppermute | solution.py:13
  156.4 8.3 %collective-permute-start = (bf16[256,128]{1,0:T(8,128)(2,1)S(1)}, bf16[256,128]{1,0:T(8,128)(2,1)S(1)}, u32[]{:S(2)}, u32[]{:S(2)}) collective-permute-start(bf16[256,128]{1,0:T(8,128)(2,1)S(1)} %get-tuple-element.374), channel_id=1, source_target_pairs={{0,16},{16,32},{32,48},{48,64},{64,80},{80,96},{96,112},{112,128},... | collective-permute-start | bytes 196616 | tf_op jit(solution)/shard_map/while/body/eval_jaxpr/ppermute | solution.py:13
  164.7 8.3 %collective-permute-start.1 = (bf16[256,128]{1,0:T(8,128)(2,1)S(1)}, bf16[256,128]{1,0:T(8,128)(2,1)S(1)}, u32[]{:S(2)}, u32[]{:S(2)}) collective-permute-start(bf16[256,128]{1,0:T(8,128)(2,1)S(1)} %get-tuple-element.375), channel_id=1, source_target_pairs={{0,16},{16,32},{32,48},{48,64},{64,80},{80,96},{96,112},{112,128},... | collective-permute-start | bytes 196616 | tf_op jit(solution)/shard_map/while/body/eval_jaxpr/ppermute | solution.py:13
  166.6 8.3 %collective-permute-start = (bf16[256,128]{1,0:T(8,128)(2,1)S(1)}, bf16[256,128]{1,0:T(8,128)(2,1)S(1)}, u32[]{:S(2)}, u32[]{:S(2)}) collective-permute-start(bf16[256,128]{1,0:T(8,128)(2,1)S(1)} %get-tuple-element.374), channel_id=1, source_target_pairs={{0,16},{16,32},{32,48},{48,64},{64,80},{80,96},{96,112},{112,128},... | collective-permute-start | bytes 196616 | tf_op jit(solution)/shard_map/while/body/eval_jaxpr/ppermute | solution.py:13
  175.0 8.3 %collective-permute-start.1 = (bf16[256,128]{1,0:T(8,128)(2,1)S(1)}, bf16[256,128]{1,0:T(8,128)(2,1)S(1)}, u32[]{:S(2)}, u32[]{:S(2)}) collective-permute-start(bf16[256,128]{1,0:T(8,128)(2,1)S(1)} %get-tuple-element.375), channel_id=1, source_target_pairs={{0,16},{16,32},{32,48},{48,64},{64,80},{80,96},{96,112},{112,128},... | collective-permute-start | bytes 196616 | tf_op jit(solution)/shard_map/while/body/eval_jaxpr/ppermute | solution.py:13
  176.9 8.3 %collective-permute-start = (bf16[256,128]{1,0:T(8,128)(2,1)S(1)}, bf16[256,128]{1,0:T(8,128)(2,1)S(1)}, u32[]{:S(2)}, u32[]{:S(2)}) collective-permute-start(bf16[256,128]{1,0:T(8,128)(2,1)S(1)} %get-tuple-element.374), channel_id=1, source_target_pairs={{0,16},{16,32},{32,48},{48,64},{64,80},{80,96},{96,112},{112,128},... | collective-permute-start | bytes 196616 | tf_op jit(solution)/shard_map/while/body/eval_jaxpr/ppermute | solution.py:13
  211.5 91.4 %all-gather.3.cloned.1.call-start = ((), (), s32[]{:S(2)}) async-start(), calls=%async_computation.4 | async-start | bytes 2785280 | tf_op jit(solution)/shard_map/all_gather | solution.py:109
  232.1 143.0 %reduce-scatter.4.cloned.1.call-start = ((), (), s32[]{:S(2)}) async-start(), calls=%async_computation.6 | async-start | bytes 2785280
  377.0 19.3 %all-to-all-start.2 = ((bf16[128,32,20]{0,2,1:T(8,128)(2,1)}), bf16[128,32,20]{0,2,1:T(8,128)(2,1)S(1)}, u32[]{:S(2)}, u32[]{:S(2)}) async-start(bf16[128,32,20]{0,2,1:T(8,128)(2,1)} %all_to_all.30), calls=%async_computation.2 | async-start | bytes 393216 | tf_op jit(solution)/shard_map/all_to_all | solution.py:130
  412.1 6.2 %collective-permute-start.3 = (bf16[256,128]{1,0:T(8,128)(2,1)S(1)}, bf16[256,128]{1,0:T(8,128)(2,1)S(1)}, u32[]{:S(2)}, u32[]{:S(2)}) collective-permute-start(bf16[256,128]{1,0:T(8,128)(2,1)S(1)} %get-tuple-element.398), channel_id=1, source_target_pairs={{16,0},{32,16},{48,32},{64,48},{80,64},{96,80},{112,96},{128,112},... | collective-permute-start | bytes 196616 | tf_op jit(solution)/shard_map/while/body/eval_jaxpr/ppermute | solution.py:13
  415.2 6.5 %collective-permute-start.2 = (bf16[256,128]{1,0:T(8,128)(2,1)S(1)}, bf16[256,128]{1,0:T(8,128)(2,1)S(1)}, u32[]{:S(2)}, u32[]{:S(2)}) collective-permute-start(bf16[256,128]{1,0:T(8,128)(2,1)S(1)} %get-tuple-element.397), channel_id=1, source_target_pairs={{16,0},{32,16},{48,32},{64,48},{80,64},{96,80},{112,96},{128,112},... | collective-permute-start | bytes 196616 | tf_op jit(solution)/shard_map/while/body/eval_jaxpr/ppermute | solution.py:13
  421.7 6.8 %collective-permute-start.3 = (bf16[256,128]{1,0:T(8,128)(2,1)S(1)}, bf16[256,128]{1,0:T(8,128)(2,1)S(1)}, u32[]{:S(2)}, u32[]{:S(2)}) collective-permute-start(bf16[256,128]{1,0:T(8,128)(2,1)S(1)} %get-tuple-element.398), channel_id=1, source_target_pairs={{16,0},{32,16},{48,32},{64,48},{80,64},{96,80},{112,96},{128,112},... | collective-permute-start | bytes 196616 | tf_op jit(solution)/shard_map/while/body/eval_jaxpr/ppermute | solution.py:13
  432.8 6.2 %collective-permute-start.3 = (bf16[256,128]{1,0:T(8,128)(2,1)S(1)}, bf16[256,128]{1,0:T(8,128)(2,1)S(1)}, u32[]{:S(2)}, u32[]{:S(2)}) collective-permute-start(bf16[256,128]{1,0:T(8,128)(2,1)S(1)} %get-tuple-element.398), channel_id=1, source_target_pairs={{16,0},{32,16},{48,32},{64,48},{80,64},{96,80},{112,96},{128,112},... | collective-permute-start | bytes 196616 | tf_op jit(solution)/shard_map/while/body/eval_jaxpr/ppermute | solution.py:13
  437.0 6.2 %collective-permute-start.2 = (bf16[256,128]{1,0:T(8,128)(2,1)S(1)}, bf16[256,128]{1,0:T(8,128)(2,1)S(1)}, u32[]{:S(2)}, u32[]{:S(2)}) collective-permute-start(bf16[256,128]{1,0:T(8,128)(2,1)S(1)} %get-tuple-element.397), channel_id=1, source_target_pairs={{16,0},{32,16},{48,32},{64,48},{80,64},{96,80},{112,96},{128,112},... | collective-permute-start | bytes 196616 | tf_op jit(solution)/shard_map/while/body/eval_jaxpr/ppermute | solution.py:13
  443.2 6.6 %collective-permute-start.3 = (bf16[256,128]{1,0:T(8,128)(2,1)S(1)}, bf16[256,128]{1,0:T(8,128)(2,1)S(1)}, u32[]{:S(2)}, u32[]{:S(2)}) collective-permute-start(bf16[256,128]{1,0:T(8,128)(2,1)S(1)} %get-tuple-element.398), channel_id=1, source_target_pairs={{16,0},{32,16},{48,32},{64,48},{80,64},{96,80},{112,96},{128,112},... | collective-permute-start | bytes 196616 | tf_op jit(solution)/shard_map/while/body/eval_jaxpr/ppermute | solution.py:13
  447.2 6.6 %collective-permute-start.2 = (bf16[256,128]{1,0:T(8,128)(2,1)S(1)}, bf16[256,128]{1,0:T(8,128)(2,1)S(1)}, u32[]{:S(2)}, u32[]{:S(2)}) collective-permute-start(bf16[256,128]{1,0:T(8,128)(2,1)S(1)} %get-tuple-element.397), channel_id=1, source_target_pairs={{16,0},{32,16},{48,32},{64,48},{80,64},{96,80},{112,96},{128,112},... | collective-permute-start | bytes 196616 | tf_op jit(solution)/shard_map/while/body/eval_jaxpr/ppermute | solution.py:13
  453.8 6.2 %collective-permute-start.3 = (bf16[256,128]{1,0:T(8,128)(2,1)S(1)}, bf16[256,128]{1,0:T(8,128)(2,1)S(1)}, u32[]{:S(2)}, u32[]{:S(2)}) collective-permute-start(bf16[256,128]{1,0:T(8,128)(2,1)S(1)} %get-tuple-element.398), channel_id=1, source_target_pairs={{16,0},{32,16},{48,32},{64,48},{80,64},{96,80},{112,96},{128,112},... | collective-permute-start | bytes 196616 | tf_op jit(solution)/shard_map/while/body/eval_jaxpr/ppermute | solution.py:13
  458.2 6.2 %collective-permute-start.2 = (bf16[256,128]{1,0:T(8,128)(2,1)S(1)}, bf16[256,128]{1,0:T(8,128)(2,1)S(1)}, u32[]{:S(2)}, u32[]{:S(2)}) collective-permute-start(bf16[256,128]{1,0:T(8,128)(2,1)S(1)} %get-tuple-element.397), channel_id=1, source_target_pairs={{16,0},{32,16},{48,32},{64,48},{80,64},{96,80},{112,96},{128,112},... | collective-permute-start | bytes 196616 | tf_op jit(solution)/shard_map/while/body/eval_jaxpr/ppermute | solution.py:13
  464.4 6.4 %collective-permute-start.3 = (bf16[256,128]{1,0:T(8,128)(2,1)S(1)}, bf16[256,128]{1,0:T(8,128)(2,1)S(1)}, u32[]{:S(2)}, u32[]{:S(2)}) collective-permute-start(bf16[256,128]{1,0:T(8,128)(2,1)S(1)} %get-tuple-element.398), channel_id=1, source_target_pairs={{16,0},{32,16},{48,32},{64,48},{80,64},{96,80},{112,96},{128,112},... | collective-permute-start | bytes 196616 | tf_op jit(solution)/shard_map/while/body/eval_jaxpr/ppermute | solution.py:13
  468.4 6.2 %collective-permute-start.2 = (bf16[256,128]{1,0:T(8,128)(2,1)S(1)}, bf16[256,128]{1,0:T(8,128)(2,1)S(1)}, u32[]{:S(2)}, u32[]{:S(2)}) collective-permute-start(bf16[256,128]{1,0:T(8,128)(2,1)S(1)} %get-tuple-element.397), channel_id=1, source_target_pairs={{16,0},{32,16},{48,32},{64,48},{80,64},{96,80},{112,96},{128,112},... | collective-permute-start | bytes 196616 | tf_op jit(solution)/shard_map/while/body/eval_jaxpr/ppermute | solution.py:13
  474.6 6.2 %collective-permute-start.3 = (bf16[256,128]{1,0:T(8,128)(2,1)S(1)}, bf16[256,128]{1,0:T(8,128)(2,1)S(1)}, u32[]{:S(2)}, u32[]{:S(2)}) collective-permute-start(bf16[256,128]{1,0:T(8,128)(2,1)S(1)} %get-tuple-element.398), channel_id=1, source_target_pairs={{16,0},{32,16},{48,32},{64,48},{80,64},{96,80},{112,96},{128,112},... | collective-permute-start | bytes 196616 | tf_op jit(solution)/shard_map/while/body/eval_jaxpr/ppermute | solution.py:13
  488.9 6.2 %collective-permute-start.2 = (bf16[256,128]{1,0:T(8,128)(2,1)S(1)}, bf16[256,128]{1,0:T(8,128)(2,1)S(1)}, u32[]{:S(2)}, u32[]{:S(2)}) collective-permute-start(bf16[256,128]{1,0:T(8,128)(2,1)S(1)} %get-tuple-element.397), channel_id=1, source_target_pairs={{16,0},{32,16},{48,32},{64,48},{80,64},{96,80},{112,96},{128,112},... | collective-permute-start | bytes 196616 | tf_op jit(solution)/shard_map/while/body/eval_jaxpr/ppermute | solution.py:13
  495.0 6.8 %collective-permute-start.3 = (bf16[256,128]{1,0:T(8,128)(2,1)S(1)}, bf16[256,128]{1,0:T(8,128)(2,1)S(1)}, u32[]{:S(2)}, u32[]{:S(2)}) collective-permute-start(bf16[256,128]{1,0:T(8,128)(2,1)S(1)} %get-tuple-element.398), channel_id=1, source_target_pairs={{16,0},{32,16},{48,32},{64,48},{80,64},{96,80},{112,96},{128,112},... | collective-permute-start | bytes 196616 | tf_op jit(solution)/shard_map/while/body/eval_jaxpr/ppermute | solution.py:13
  499.1 6.2 %collective-permute-start.2 = (bf16[256,128]{1,0:T(8,128)(2,1)S(1)}, bf16[256,128]{1,0:T(8,128)(2,1)S(1)}, u32[]{:S(2)}, u32[]{:S(2)}) collective-permute-start(bf16[256,128]{1,0:T(8,128)(2,1)S(1)} %get-tuple-element.397), channel_id=1, source_target_pairs={{16,0},{32,16},{48,32},{64,48},{80,64},{96,80},{112,96},{128,112},... | collective-permute-start | bytes 196616 | tf_op jit(solution)/shard_map/while/body/eval_jaxpr/ppermute | solution.py:13
  505.3 6.2 %collective-permute-start.3 = (bf16[256,128]{1,0:T(8,128)(2,1)S(1)}, bf16[256,128]{1,0:T(8,128)(2,1)S(1)}, u32[]{:S(2)}, u32[]{:S(2)}) collective-permute-start(bf16[256,128]{1,0:T(8,128)(2,1)S(1)} %get-tuple-element.398), channel_id=1, source_target_pairs={{16,0},{32,16},{48,32},{64,48},{80,64},{96,80},{112,96},{128,112},... | collective-permute-start | bytes 196616 | tf_op jit(solution)/shard_map/while/body/eval_jaxpr/ppermute | solution.py:13
  509.3 6.6 %collective-permute-start.2 = (bf16[256,128]{1,0:T(8,128)(2,1)S(1)}, bf16[256,128]{1,0:T(8,128)(2,1)S(1)}, u32[]{:S(2)}, u32[]{:S(2)}) collective-permute-start(bf16[256,128]{1,0:T(8,128)(2,1)S(1)} %get-tuple-element.397), channel_id=1, source_target_pairs={{16,0},{32,16},{48,32},{64,48},{80,64},{96,80},{112,96},{128,112},... | collective-permute-start | bytes 196616 | tf_op jit(solution)/shard_map/while/body/eval_jaxpr/ppermute | solution.py:13
  516.0 6.2 %collective-permute-start.3 = (bf16[256,128]{1,0:T(8,128)(2,1)S(1)}, bf16[256,128]{1,0:T(8,128)(2,1)S(1)}, u32[]{:S(2)}, u32[]{:S(2)}) collective-permute-start(bf16[256,128]{1,0:T(8,128)(2,1)S(1)} %get-tuple-element.398), channel_id=1, source_target_pairs={{16,0},{32,16},{48,32},{64,48},{80,64},{96,80},{112,96},{128,112},... | collective-permute-start | bytes 196616 | tf_op jit(solution)/shard_map/while/body/eval_jaxpr/ppermute | solution.py:13
  519.5 6.2 %collective-permute-start.2 = (bf16[256,128]{1,0:T(8,128)(2,1)S(1)}, bf16[256,128]{1,0:T(8,128)(2,1)S(1)}, u32[]{:S(2)}, u32[]{:S(2)}) collective-permute-start(bf16[256,128]{1,0:T(8,128)(2,1)S(1)} %get-tuple-element.397), channel_id=1, source_target_pairs={{16,0},{32,16},{48,32},{64,48},{80,64},{96,80},{112,96},{128,112},... | collective-permute-start | bytes 196616 | tf_op jit(solution)/shard_map/while/body/eval_jaxpr/ppermute | solution.py:13
  525.7 6.2 %collective-permute-start.3 = (bf16[256,128]{1,0:T(8,128)(2,1)S(1)}, bf16[256,128]{1,0:T(8,128)(2,1)S(1)}, u32[]{:S(2)}, u32[]{:S(2)}) collective-permute-start(bf16[256,128]{1,0:T(8,128)(2,1)S(1)} %get-tuple-element.398), channel_id=1, source_target_pairs={{16,0},{32,16},{48,32},{64,48},{80,64},{96,80},{112,96},{128,112},... | collective-permute-start | bytes 196616 | tf_op jit(solution)/shard_map/while/body/eval_jaxpr/ppermute | solution.py:13
  529.8 6.2 %collective-permute-start.2 = (bf16[256,128]{1,0:T(8,128)(2,1)S(1)}, bf16[256,128]{1,0:T(8,128)(2,1)S(1)}, u32[]{:S(2)}, u32[]{:S(2)}) collective-permute-start(bf16[256,128]{1,0:T(8,128)(2,1)S(1)} %get-tuple-element.397), channel_id=1, source_target_pairs={{16,0},{32,16},{48,32},{64,48},{80,64},{96,80},{112,96},{128,112},... | collective-permute-start | bytes 196616 | tf_op jit(solution)/shard_map/while/body/eval_jaxpr/ppermute | solution.py:13
  536.0 7.0 %collective-permute-start.3 = (bf16[256,128]{1,0:T(8,128)(2,1)S(1)}, bf16[256,128]{1,0:T(8,128)(2,1)S(1)}, u32[]{:S(2)}, u32[]{:S(2)}) collective-permute-start(bf16[256,128]{1,0:T(8,128)(2,1)S(1)} %get-tuple-element.398), channel_id=1, source_target_pairs={{16,0},{32,16},{48,32},{64,48},{80,64},{96,80},{112,96},{128,112},... | collective-permute-start | bytes 196616 | tf_op jit(solution)/shard_map/while/body/eval_jaxpr/ppermute | solution.py:13
  540.6 6.7 %collective-permute-start.2 = (bf16[256,128]{1,0:T(8,128)(2,1)S(1)}, bf16[256,128]{1,0:T(8,128)(2,1)S(1)}, u32[]{:S(2)}, u32[]{:S(2)}) collective-permute-start(bf16[256,128]{1,0:T(8,128)(2,1)S(1)} %get-tuple-element.397), channel_id=1, source_target_pairs={{16,0},{32,16},{48,32},{64,48},{80,64},{96,80},{112,96},{128,112},... | collective-permute-start | bytes 196616 | tf_op jit(solution)/shard_map/while/body/eval_jaxpr/ppermute | solution.py:13
  547.3 6.2 %collective-permute-start.3 = (bf16[256,128]{1,0:T(8,128)(2,1)S(1)}, bf16[256,128]{1,0:T(8,128)(2,1)S(1)}, u32[]{:S(2)}, u32[]{:S(2)}) collective-permute-start(bf16[256,128]{1,0:T(8,128)(2,1)S(1)} %get-tuple-element.398), channel_id=1, source_target_pairs={{16,0},{32,16},{48,32},{64,48},{80,64},{96,80},{112,96},{128,112},... | collective-permute-start | bytes 196616 | tf_op jit(solution)/shard_map/while/body/eval_jaxpr/ppermute | solution.py:13
  551.4 6.2 %collective-permute-start.2 = (bf16[256,128]{1,0:T(8,128)(2,1)S(1)}, bf16[256,128]{1,0:T(8,128)(2,1)S(1)}, u32[]{:S(2)}, u32[]{:S(2)}) collective-permute-start(bf16[256,128]{1,0:T(8,128)(2,1)S(1)} %get-tuple-element.397), channel_id=1, source_target_pairs={{16,0},{32,16},{48,32},{64,48},{80,64},{96,80},{112,96},{128,112},... | collective-permute-start | bytes 196616 | tf_op jit(solution)/shard_map/while/body/eval_jaxpr/ppermute | solution.py:13
  557.6 6.2 %collective-permute-start.3 = (bf16[256,128]{1,0:T(8,128)(2,1)S(1)}, bf16[256,128]{1,0:T(8,128)(2,1)S(1)}, u32[]{:S(2)}, u32[]{:S(2)}) collective-permute-start(bf16[256,128]{1,0:T(8,128)(2,1)S(1)} %get-tuple-element.398), channel_id=1, source_target_pairs={{16,0},{32,16},{48,32},{64,48},{80,64},{96,80},{112,96},{128,112},... | collective-permute-start | bytes 196616 | tf_op jit(solution)/shard_map/while/body/eval_jaxpr/ppermute | solution.py:13
  561.7 6.2 %collective-permute-start.2 = (bf16[256,128]{1,0:T(8,128)(2,1)S(1)}, bf16[256,128]{1,0:T(8,128)(2,1)S(1)}, u32[]{:S(2)}, u32[]{:S(2)}) collective-permute-start(bf16[256,128]{1,0:T(8,128)(2,1)S(1)} %get-tuple-element.397), channel_id=1, source_target_pairs={{16,0},{32,16},{48,32},{64,48},{80,64},{96,80},{112,96},{128,112},... | collective-permute-start | bytes 196616 | tf_op jit(solution)/shard_map/while/body/eval_jaxpr/ppermute | solution.py:13
  567.8 6.2 %collective-permute-start.3 = (bf16[256,128]{1,0:T(8,128)(2,1)S(1)}, bf16[256,128]{1,0:T(8,128)(2,1)S(1)}, u32[]{:S(2)}, u32[]{:S(2)}) collective-permute-start(bf16[256,128]{1,0:T(8,128)(2,1)S(1)} %get-tuple-element.398), channel_id=1, source_target_pairs={{16,0},{32,16},{48,32},{64,48},{80,64},{96,80},{112,96},{128,112},... | collective-permute-start | bytes 196616 | tf_op jit(solution)/shard_map/while/body/eval_jaxpr/ppermute | solution.py:13
  (14 other events, 306.2 us)
Sparse Core Ops, SparseCore 0:
  211.7 44.0 all-gather.4
  258.3 44.5 all-gather.2
  313.7 61.4 reduce-scatter.3
where the time goes:
time: 590 us; the launch traced here: 585 us
  waiting for transfers between devices  279 us (47%)
  starting transfers between devices  181 us (31%)
  matrix products  35.4 us (6%)
  blocking collectives  30.7 us (5%)
  local copies, waits for them, and re-layouts  21.9 us (4%)
  other arithmetic  21.3 us (4%)
  between operations  14.7 us (2%)
    ppermute x64, starting transfers between devices, shifted(): return lax.ppermute(block, axis, route)  170 us
    ppermute x64, waiting for transfers between devices, shifted(): return lax.ppermute(block, axis, route)  149 us
    unnamed x4, waiting for transfers between devices  57.7 us
    all_gather x1, waiting for transfers between devices, per_device(): full_grads = lax.all_gather(recv_grads, 'exp', axis=1, tiled=True)  43.8 us
    all_gather x1, waiting for transfers between devices, per_device(): full_tokens = lax.all_gather(recv_tokens, 'exp', axis=1, tiled=True)  23.5 us
    all_to_all x1, blocking collectives, per_device(): lax.all_to_all(send_grads, 'seq', split_axis=0, concat_axis=0, tiled=True)  15.9 us
    all_to_all x1, blocking collectives, per_device(): lax.all_to_all(send_tokens, 'seq', split_axis=0, concat_axis=0, tiled=True)  14.9 us
    add x16, other arithmetic, relay_grads(): value_acc + lax.dynamic_index_in_dim(value_parts, index, 0, keepdims=False)  14.7 us
  transfers between devices with their start and end apart: 68, of which 64 were waited for; matrix products, arithmetic and copies ran while one was open for 5% of the time, Pallas kernels for 0%

commit v1 on v0

v1 whole, which is shorter than its diff:
```python
import functools

import jax
import jax.numpy as jnp
from jax import lax
from jax.experimental import pallas as pl
from jax.experimental.pallas import tpu as pltpu
from jax.sharding import PartitionSpec as P

HD = 128
WCH = 16
PAD = 32
F32 = jnp.float32
BF16 = jnp.bfloat16
MESH = pl.DeviceIdType.MESH
NEG = -1.0e30


def nt(a, b):
    return lax.dot_general(a, b, (((1,), (1,)), ((), ())), preferred_element_type=F32)


def nn(a, b):
    return lax.dot_general(a, b, (((1,), (0,)), ((), ())), preferred_element_type=F32)


def tn(a, b):
    return lax.dot_general(a, b, (((0,), (0,)), ((), ())), preferred_element_type=F32)


def transposed(a):
    return jnp.transpose(a.astype(F32)).astype(BF16)


def remote(src, dst, send_sem, recv_sem, device):
    return pltpu.make_async_remote_copy(
        src_ref=src,
        dst_ref=dst,
        send_sem=send_sem,
        recv_sem=recv_sem,
        device_id=device,
        device_id_type=MESH,
    )


class GatherRing:
    def __init__(self, count, me, device_of, view, sems, on_arrival=None):
        self.n, self.me, self.view, self.on_arrival = count, me, view, on_arrival
        self.half = count // 2
        self.right = device_of(lax.rem(me + 1, count))
        self.left = device_of(lax.rem(me + count - 1, count))
        self.sems = sems

    def block(self, direction, hops):
        return lax.rem(self.me + (self.n - hops if direction == 0 else hops), self.n)

    def sends(self, direction, k, part):
        return k < self.half - 1 or (k == self.half - 1 and part == direction)

    def copy(self, direction, k, part, hops):
        ref = self.view(self.block(direction, hops), part)
        i = 2 * k + part
        return remote(
            ref,
            ref,
            self.sems[2 * direction].at[i],
            self.sems[2 * direction + 1].at[i],
            self.right if direction == 0 else self.left,
        )

    def start(self):
        for part in range(2):
            for direction in range(2):
                if self.sends(direction, 0, part):
                    self.copy(direction, 0, part, 0).start()
        if self.on_arrival:
            for part in range(2):
                self.on_arrival(self.me, 0, part)

    def step(self, k, part):
        for direction in range(2):
            if not self.sends(direction, k - 1, part):
                continue
            self.copy(direction, k - 1, part, k).wait_recv()
            if self.sends(direction, k, part):
                self.copy(direction, k, part, k).start()
            if self.on_arrival:
                distance = (self.n - k if direction == 0 else k) % self.n
                self.on_arrival(self.block(direction, k), distance, part)

    def drain(self):
        for k in range(self.half):
            for part in range(2):
                for direction in range(2):
                    if self.sends(direction, k, part):
                        self.copy(direction, k, part, k).wait_send()


def scratch_table(E, Y, Z, BL, D, FL, CAP):
    R, RP, hz, hy = E * CAP, E * PAD, max(Z // 2, 1), max(Y // 2, 1)
    table = dict(
        k3=((3, BL, HD), BF16),
        v3=((3, BL, HD), BF16),
        kt3=((3, HD, BL), BF16),
        vt3=((3, HD, BL), BF16),
        qb=((Z, BL, HD), BF16),
        gb=((Z, BL, HD), BF16),
        cb=((BL, BL), F32),
        osend=((Z, HD, BL), BF16),
        orecv=((Z, HD, BL), BF16),
        lsend=((Z, 8, BL), F32),
        lrecv=((Z, 8, BL), F32),
        stats=((Z, 16, BL), F32),
        ot=((HD, BL), BF16),
        ogt=((HD, BL), F32),
        routing=((RP, 2 * BL), BF16),
        comp=((R, RP), BF16),
        compt=((RP, R), BF16),
        gs=((E, PAD, HD), BF16),
        gr=((E, PAD, HD), BF16),
        ts=((E, PAD, HD), BF16),
        tr=((E, PAD, HD), BF16),
        bs=((E, PAD, HD), BF16),
        br=((E, PAD, HD), BF16),
        grads=((2 * Y, R, HD), BF16),
        toks=((2 * Y, R, HD), BF16),
        win=((D, FL), BF16),
        wout=((FL, D), BF16),
        thr=((R, FL), F32),
        pre=((R, FL), F32),
        hid=((FL, R), BF16),
        hg=((R, FL), BF16),
        pb=((Y, R, HD), BF16),
        sb=((Y, R, HD), BF16),
        rb=((Y, R, HD), BF16),
        rs_stage=((2, 2 * hy, R // 2, HD), BF16),
        rs_recv=((2, 2 * hy, R // 2, HD), BF16),
        dwi=((D, FL), BF16),
        dwo=((FL, D), BF16),
        dk3=((3, BL, HD), F32),
        dv3=((3, BL, HD), F32),
        dksend=((2, BL, HD), BF16),
        dvsend=((2, BL, HD), BF16),
        dkrecv=((2, BL, HD), BF16),
        dvrecv=((2, BL, HD), BF16),
        dqsend=((Z, HD, BL), BF16),
        dqrecv=((Z, HD, BL), BF16),
        dqown=((HD, BL), F32),
    )
    shapes = {name: pltpu.VMEM(shape, dtype) for name, (shape, dtype) in table.items()}
    counts = dict(
        kv_s=4, kv_r=4, o_s=Z, o_r=Z, l_s=Z, l_r=Z, st_s=Z, st_r=Z, dq_s=Z, dq_r=Z, dkv_s=4, dkv_r=4,
        ga_s=E, ga_r=E, ta_s=E, ta_r=E, ba_s=E, ba_r=E, w=2, dw=2,
        gsib_s=2 * Y, gsib_r=2 * Y, tsib_s=2 * Y, tsib_r=2 * Y, psib_s=Y, psib_r=Y,
    )
    for ring, half in (("q", hz), ("g", hz), ("ygr", hy), ("ytk", hy), ("rs", hy)):
        for end in ("_rs", "_rr", "_ls", "_lr"):
            counts[ring + end] = 2 * half
    for name, count in counts.items():
        shapes["sem_" + name] = pltpu.SemaphoreType.DMA((count,))
    return shapes


def body(names, E, Y, Z, CAP, *refs):
    (q_ref, k_ref, v_ref, og_ref, ids_ref, gates_ref, slope_ref, win_ref, wout_ref,
     dq_ref, dk_ref, dv_ref, dwi_ref, dwo_ref) = refs[:14]
    S = dict(zip(names, refs[14:]))
    BL, FL = q_ref.shape[0], win_ref.shape[2]
    X, R, RP, D = E // Z, E * CAP, E * PAD, 2 * Y * HD
    scale = HD ** (-0.5)
    s, e = lax.axis_index("seq"), lax.axis_index("exp")
    x, z = lax.div(s, Z), lax.rem(s, Z)
    y, c = lax.div(e, 2), lax.rem(e, 2)
    sibling = (s, 2 * y + 1 - c)

    def zdev(j):
        return (x * Z + j, e)

    def xdev(i):
        return (lax.rem(i, X) * Z + z, e)

    def ydev(j):
        return (s, 2 * j + c)

    weights_in = [
        pltpu.make_async_copy(win_ref.at[0], S["win"], S["sem_w"].at[0]),
        pltpu.make_async_copy(wout_ref.at[0], S["wout"], S["sem_w"].at[1]),
    ]
    for copy in weights_in:
        copy.start()

    barrier = pltpu.get_barrier_semaphore()

    def greet(i, carry):
        pl.semaphore_signal(
            barrier, inc=1, device_id=(lax.rem(s + i, E), e), device_id_type=MESH
        )
        return carry

    lax.fori_loop(1, E, greet, 0)
    for device in (ydev(lax.rem(y + 1, Y)), ydev(lax.rem(y + Y - 1, Y)), sibling):
        pl.semaphore_signal(barrier, inc=1, device_id=device, device_id_type=MESH)

    S["qb"][z] = q_ref[...]
    S["k3"][0] = k_ref[...]
    S["v3"][0] = v_ref[...]
    S["kt3"][0] = transposed(k_ref[...])
    S["vt3"][0] = transposed(v_ref[...])
    pl.semaphore_wait(barrier, E - 1 + 3)

    q_ring = GatherRing(
        Z, z, zdev, lambda b, p: S["qb"].at[b, pl.ds(p * (BL // 2), BL // 2), :],
        [S["sem_q_rs"], S["sem_q_rr"], S["sem_q_ls"], S["sem_q_lr"]],
    )
    q_ring.start()
    kv_copies = []
    for hop in (1, 2):
        for which, (own, buf) in enumerate((("k3", "k3"), ("v3", "v3"))):
            i = 2 * (hop - 1) + which
            copy = remote(
                S[own].at[0], S[buf].at[hop], S["sem_kv_s"].at[i], S["sem_kv_r"].at[i],
                xdev(x + hop),
            )
            copy.start()
            kv_copies.append(copy)

    flat = jnp.concatenate([ids_ref[0:1, :], ids_ref[1:2, :]], axis=1)
    hot = lax.broadcasted_iota(jnp.int32, (E, 2 * BL), 0) == flat
    hot_f = jnp.where(hot, 1.0, 0.0)
    upper = lax.broadcasted_iota(jnp.int32, (2 * BL, 2 * BL), 0) < lax.broadcasted_iota(
        jnp.int32, (2 * BL, 2 * BL), 1
    )
    before = nn(hot_f.astype(BF16), jnp.where(upper, 1.0, 0.0).astype(BF16))
    position = jnp.sum(before * hot_f, axis=0, keepdims=True)
    slot = jnp.where(position < CAP, flat * PAD + position.astype(jnp.int32), -1)
    S["routing"][...] = jnp.where(
        lax.broadcasted_iota(jnp.int32, (RP, 2 * BL), 0) == slot, 1.0, 0.0
    ).astype(BF16)
    ogt = jnp.transpose(og_ref[...].astype(F32))
    S["ogt"][...] = ogt
    scaled = jnp.concatenate([ogt * gates_ref[0:1, :], ogt * gates_ref[1:2, :]], axis=1)
    S["gs"][...] = nt(S["routing"][...], scaled.astype(BF16)).astype(BF16).reshape(E, PAD, HD)

    def exchange_start(send, recv, send_sem, recv_sem):
        recv[s] = send[s]

        def go(i, carry):
            peer = lax.rem(s + i, E)
            remote(send.at[peer], recv.at[s], send_sem.at[i], recv_sem.at[i], (peer, e)).start()
            return carry

        lax.fori_loop(1, E, go, 0)

    def exchange_wait(send, recv, send_sem, recv_sem):
        def go(i, carry):
            peer = lax.rem(s + E - i, E)
            remote(send.at[peer], recv.at[peer], send_sem.at[i], recv_sem.at[i], (peer, e)).wait_recv()
            return carry

        lax.fori_loop(1, E, go, 0)

    def exchange_drain(send, recv, send_sem, recv_sem):
        def go(i, carry):
            peer = lax.rem(s + i, E)
            remote(send.at[peer], recv.at[s], send_sem.at[i], recv_sem.at[i], (peer, e)).wait_send()
            return carry

        lax.fori_loop(1, E, go, 0)

    grad_exchange = (S["gs"], S["gr"], S["sem_ga_s"], S["sem_ga_r"])
    token_exchange = (S["ts"], S["tr"], S["sem_ta_s"], S["sem_ta_r"])
    back_exchange = (S["bs"], S["br"], S["sem_ba_s"], S["sem_ba_r"])
    exchange_start(*grad_exchange)

    padded = lax.broadcasted_iota(jnp.int32, (1, RP), 1)
    packed_of = jnp.where(
        (padded & (PAD - 1)) < CAP, (padded >> 5) * CAP + (padded & (PAD - 1)), -1
    )
    S["comp"][...] = jnp.where(
        lax.broadcasted_iota(jnp.int32, (R, RP), 0) == packed_of, 1.0, 0.0
    ).astype(BF16)

    slope = slope_ref[0]
    S["cb"][...] = lax.broadcasted_iota(jnp.int32, (BL, BL), 0).astype(F32) * slope
    causal = lax.broadcasted_iota(jnp.int32, (BL, BL), 0) <= lax.broadcasted_iota(
        jnp.int32, (BL, BL), 1
    )

    def pieces(d, j):
        def offset(r):
            distance = ((j - z) * BL).astype(F32) + float(r * Z * BL)
            return jnp.where(x >= r, 0.0, NEG) - slope * distance

        if d == 0:
            return [(0, offset(0), causal), (1, offset(1), None), (2, offset(2), ~causal)]
        r = jnp.where(j > z, 0, 2)
        near = jnp.where(j > z, offset(0), offset(2))
        return [(r, near, None), (1, offset(1), None)]

    def scores_of(r, offset, mask, queries):
        raw = nt(S["k3"][r], queries) * scale + (S["cb"][...] + offset)
        return raw if mask is None else jnp.where(mask, raw, NEG)

    def forward(d):
        j = lax.rem(z + d, Z)
        queries = S["qb"][j]
        parts = pieces(d, j)
        scores = [scores_of(r, offset, mask, queries) for r, offset, mask in parts]
        top = functools.reduce(
            jnp.maximum, [jnp.max(t, axis=0, keepdims=True) for t in scores]
        )
        total, out = 0.0, 0.0
        for (r, _, _), t in zip(parts, scores):
            p = jnp.exp(t - top)
            total = total + jnp.sum(p, axis=0, keepdims=True)
            out = out + nn(S["vt3"][r], p.astype(BF16))
        out = (out / total).astype(BF16)
        log_norm = jnp.broadcast_to(top + jnp.log(total), (8, BL))
        if d == 0:
            S["orecv"][0] = out
            S["lrecv"][0] = log_norm
            return
        S["osend"][d] = out
        S["lsend"][d] = log_norm
        out_copy(d).start()
        norm_copy(d).start()

    def out_copy(d):
        return remote(S["osend"].at[d], S["orecv"].at[d], S["sem_o_s"].at[d], S["sem_o_r"].at[d],
                      zdev(lax.rem(z + d, Z)))

    def norm_copy(d):
        return remote(S["lsend"].at[d], S["lrecv"].at[d], S["sem_l_s"].at[d], S["sem_l_r"].at[d],
                      zdev(lax.rem(z + d, Z)))

    for copy in kv_copies:
        copy.wait_recv()
    for r in (1, 2):
        S["kt3"][r] = transposed(S["k3"][r])
        S["vt3"][r] = transposed(S["v3"][r])
    forward(0)

    def feature_ring(buf, ring, sib):
        def arrived(block, distance, part):
            sib_copy(buf, sib, block, distance, part).start()

        return GatherRing(
            Y, y, ydev, lambda b, p: buf.at[2 * b + c, pl.ds(p * (R // 2), R // 2), :],
            [S["sem_" + ring + end] for end in ("_rs", "_rr", "_ls", "_lr")], arrived,
        )

    def sib_copy(buf, sib, block, distance, part):
        ref = buf.at[2 * block + c, pl.ds(part * (R // 2), R // 2), :]
        i = 2 * distance + part
        return remote(ref, ref, S["sem_" + sib + "_s"].at[i], S["sem_" + sib + "_r"].at[i], sibling)

    def sib_wait(buf, sib, distance):
        block = lax.rem(y + distance, Y)
        for part in range(2):
            ref = buf.at[2 * block + 1 - c, pl.ds(part * (R // 2), R // 2), :]
            i = 2 * distance + part
            remote(ref, ref, S["sem_" + sib + "_s"].at[i], S["sem_" + sib + "_r"].at[i], sibling).wait_recv()

    def sib_drain(buf, sib):
        for distance in range(Y):
            for part in range(2):
                sib_copy(buf, sib, lax.rem(y + distance, Y), distance, part).wait_send()

    exchange_wait(*grad_exchange)
    S["grads"][e] = nn(S["comp"][...], S["gr"][...].reshape(RP, HD)).astype(BF16)
    grad_ring = feature_ring(S["grads"], "ygr", "gsib")
    grad_ring.start()
    grad_steps = [(k, p) for k in range(1, Y // 2 + 1) for p in range(2)]

    def advance_grads():
        if grad_steps:
            grad_ring.step(*grad_steps.pop(0))

    for k in range(1, Z // 2 + 1):
        for part in range(2):
            q_ring.step(k, part)
        for d in sorted({k, Z - k}):
            forward(d)
        advance_grads()

    for d in range(1, Z):
        out_copy(d).wait_recv()
        norm_copy(d).wait_recv()
    norms = [S["lrecv"][d][0:1, :] for d in range(Z)]
    top = functools.reduce(jnp.maximum, norms)
    shares = [jnp.exp(t - top) for t in norms]
    total = functools.reduce(jnp.add, shares)
    merged = functools.reduce(
        jnp.add, [S["orecv"][d].astype(F32) * shares[d] for d in range(Z)]
    )
    out_t = (merged / total).astype(BF16)
    S["ot"][...] = out_t
    log_norm = top + jnp.log(total)
    S["stats"][z, 0:8, :] = jnp.broadcast_to(log_norm, (8, BL))

    S["ts"][...] = (
        nt(S["routing"][...], jnp.concatenate([out_t, out_t], axis=1))
        .astype(BF16)
        .reshape(E, PAD, HD)
    )
    exchange_start(*token_exchange)

    def pair(buf, block):
        return jnp.concatenate([buf[2 * block], buf[2 * block + 1]], axis=1)

    def columns(block):
        return pl.ds(pl.multiple_of(block * (2 * HD), 2 * HD), 2 * HD)

    order = [0]
    for k in range(1, Y // 2 + 1):
        order += sorted({k, Y - k})

    for copy in weights_in:
        copy.wait()
    while grad_steps:
        advance_grads()
    for n, d in enumerate(order):
        sib_wait(S["grads"], "gsib", d)
        block = lax.rem(y + d, Y)
        term = nt(pair(S["grads"], block), S["wout"][:, columns(block)])
        S["thr"][...] = term if n == 0 else S["thr"][...] + term

    exchange_wait(*token_exchange)
    S["toks"][e] = nn(S["comp"][...], S["tr"][...].reshape(RP, HD)).astype(BF16)
    token_ring = feature_ring(S["toks"], "ytk", "tsib")
    token_ring.start()
    slots = lax.broadcasted_iota(jnp.int32, (RP, R), 0)
    packed_rows = jnp.where(
        (slots & (PAD - 1)) < CAP, (slots >> 5) * CAP + (slots & (PAD - 1)), -1
    )
    S["compt"][...] = jnp.where(
        packed_rows == lax.broadcasted_iota(jnp.int32, (RP, R), 1), 1.0, 0.0
    ).astype(BF16)

    def pre_term(d):
        sib_wait(S["toks"], "tsib", d)
        block = lax.rem(y + d, Y)
        term = nn(pair(S["toks"], block), S["win"][columns(block), :])
        S["pre"][...] = term if d == 0 else S["pre"][...] + term

    pre_term(0)
    for k in range(1, Y // 2 + 1):
        for part in range(2):
            token_ring.step(k, part)
        for d in sorted({k, Y - k}):
            pre_term(d)

    pre = S["pre"][...]
    logistic = 1.0 / (1.0 + jnp.exp(-pre))
    S["hid"][...] = jnp.transpose(pre * logistic).astype(BF16)
    S["hg"][...] = (S["thr"][...] * logistic * (1.0 + pre * (1.0 - logistic))).astype(BF16)

    def partner_copy(distance):
        block = lax.rem(y + distance, Y)
        return remote(S["sb"].at[block], S["rb"].at[block], S["sem_psib_s"].at[distance],
                      S["sem_psib_r"].at[distance], sibling)

    far_first = order[::-1]
    for d in far_first:
        block = lax.rem(y + d, Y)
        share = nt(S["hg"][...], S["win"][columns(block), :]).astype(BF16)
        first, second = share[:, :HD], share[:, HD:]
        S["pb"][block] = jnp.where(c == 0, first, second)
        S["sb"][block] = jnp.where(c == 0, second, first)
        partner_copy(d).start()

    half = Y // 2
    rows = R // 2

    def hops(direction, chunk):
        return half if direction == chunk else half - 1

    def ring_copy(direction, chunk, h):
        i = 2 * h + chunk
        ends = ("_rs", "_rr") if direction == 0 else ("_ls", "_lr")
        neighbour = ydev(lax.rem(y + 1, Y)) if direction == 0 else ydev(lax.rem(y + Y - 1, Y))
        return remote(S["rs_stage"].at[direction, i], S["rs_recv"].at[direction, i],
                      S["sem_rs" + ends[0]].at[i], S["sem_rs" + ends[1]].at[i], neighbour)

    def own_part(block, chunk):
        span = pl.ds(chunk * rows, rows)
        return S["pb"][block, span, :].astype(F32) + S["rb"][block, span, :].astype(F32)

    weight_work = [("out", d) for d in order] + [("in", d) for d in order]

    def some_weight_work(count):
        for _ in range(min(count, len(weight_work))):
            which, d = weight_work.pop(0)
            block = lax.rem(y + d, Y)
            if which == "out":
                S["dwo"][:, columns(block)] = nn(S["hid"][...], pair(S["grads"], block)).astype(BF16)
            else:
                S["dwi"][columns(block), :] = tn(pair(S["toks"], block), S["hg"][...]).astype(BF16)

    waited = set()

    def need_partner(distance):
        if distance not in waited:
            waited.add(distance)
            partner_copy(distance).wait_recv()

    per_hop = -(-2 * Y // half)
    for h in range(half):
        for direction, chunk in ((0, 0), (1, 1), (0, 1), (1, 0)):
            total_hops = hops(direction, chunk)
            if h >= total_hops:
                continue
            distance = total_hops - h if direction == 0 else Y - (total_hops - h)
            need_partner(distance)
            value = own_part(lax.rem(y + distance, Y), chunk)
            if h > 0:
                ring_copy(direction, chunk, h - 1).wait_recv()
                value = value + S["rs_recv"][direction, 2 * (h - 1) + chunk].astype(F32)
            S["rs_stage"][direction, 2 * h + chunk] = value.astype(BF16)
            ring_copy(direction, chunk, h).start()
        some_weight_work(per_hop)
    need_partner(0)
    sums = []
    for chunk in range(2):
        value = own_part(y, chunk)
        for direction in range(2):
            last = hops(direction, chunk) - 1
            if last >= 0:
                ring_copy(direction, chunk, last).wait_recv()
                value = value + S["rs_recv"][direction, 2 * last + chunk].astype(F32)
        sums.append(value.astype(BF16))
    back = jnp.concatenate(sums, axis=0)
    S["bs"][...] = nn(S["compt"][...], back).astype(BF16).reshape(E, PAD, HD)
    exchange_start(*back_exchange)
    some_weight_work(2 * Y)
    weights_out = [
        pltpu.make_async_copy(S["dwi"], dwi_ref.at[0], S["sem_dw"].at[0]),
        pltpu.make_async_copy(S["dwo"], dwo_ref.at[0], S["sem_dw"].at[1]),
    ]
    for copy in weights_out:
        copy.start()
    exchange_wait(*back_exchange)
    combined = tn(S["br"][...].reshape(RP, HD), S["routing"][...])
    grad_t = (S["ogt"][...] + combined[:, :BL] + combined[:, BL:]).astype(BF16).astype(F32)
    delta = jnp.sum(grad_t * S["ot"][...].astype(F32), axis=0, keepdims=True)
    S["stats"][z, 8:16, :] = jnp.broadcast_to(delta, (8, BL))
    S["gb"][z] = jnp.transpose(grad_t).astype(BF16)

    g_ring = GatherRing(
        Z, z, zdev, lambda b, p: S["gb"].at[b, pl.ds(p * (BL // 2), BL // 2), :],
        [S["sem_g_rs"], S["sem_g_rr"], S["sem_g_ls"], S["sem_g_lr"]],
    )

    def stats_copy(d, block):
        ref = S["stats"].at[block]
        return remote(ref, ref, S["sem_st_s"].at[d], S["sem_st_r"].at[d], zdev(lax.rem(z + d, Z)))

    for d in range(1, Z):
        stats_copy(d, z).start()
    g_ring.start()

    def dq_copy(d):
        return remote(S["dqsend"].at[d], S["dqrecv"].at[d], S["sem_dq_s"].at[d], S["sem_dq_r"].at[d],
                      zdev(lax.rem(z + d, Z)))

    def backward(d):
        j = lax.rem(z + d, Z)
        queries, grads = S["qb"][j], S["gb"][j]
        norm, dlt = S["stats"][j, 0:1, :], S["stats"][j, 8:9, :]
        dq = 0.0
        for r, offset, mask in pieces(d, j):
            p = jnp.exp(scores_of(r, offset, mask, queries) - norm)
            dv = nn(p.astype(BF16), grads)
            ds = (p * (nt(S["v3"][r], grads) - dlt)).astype(BF16)
            dk = nn(ds, queries)
            dq = dq + nn(S["kt3"][r], ds)
            if d == 0:
                S["dv3"][r], S["dk3"][r] = dv, dk
            else:
                S["dv3"][r] = S["dv3"][r] + dv
                S["dk3"][r] = S["dk3"][r] + dk
        dq = dq * scale
        if d == 0:
            S["dqown"][...] = dq
        else:
            S["dqsend"][d] = dq.astype(BF16)
            dq_copy(d).start()

    backward(0)
    for k in range(1, Z // 2 + 1):
        for part in range(2):
            g_ring.step(k, part)
        for d in sorted({k, Z - k}):
            stats_copy(Z - d, lax.rem(z + d, Z)).wait_recv()
            backward(d)

    dkv_copies = []
    for hop in (1, 2):
        S["dksend"][hop - 1] = (S["dk3"][hop] * scale).astype(BF16)
        S["dvsend"][hop - 1] = S["dv3"][hop].astype(BF16)
        for which, name in enumerate(("dk", "dv")):
            i = 2 * (hop - 1) + which
            copy = remote(S[name + "send"].at[hop - 1], S[name + "recv"].at[hop - 1],
                          S["sem_dkv_s"].at[i], S["sem_dkv_r"].at[i], xdev(x + X - hop))
            copy.start()
            dkv_copies.append(copy)

    dq = S["dqown"][...]
    for d in range(1, Z):
        dq_copy(d).wait_recv()
        dq = dq + S["dqrecv"][d].astype(F32)
    dq_ref[...] = jnp.transpose(dq).astype(BF16)
    for copy in dkv_copies:
        copy.wait_recv()
    dk_ref[...] = (
        S["dk3"][0] * scale + S["dkrecv"][0].astype(F32) + S["dkrecv"][1].astype(F32)
    ).astype(BF16)
    dv_ref[...] = (
        S["dv3"][0] + S["dvrecv"][0].astype(F32) + S["dvrecv"][1].astype(F32)
    ).astype(BF16)

    for copy in kv_copies + dkv_copies:
        copy.wait_send()
    for ring in (q_ring, g_ring, grad_ring, token_ring):
        ring.drain()
    for d in range(1, Z):
        out_copy(d).wait_send()
        norm_copy(d).wait_send()
        stats_copy(d, z).wait_send()
        dq_copy(d).wait_send()
    for exchange in (grad_exchange, token_exchange, back_exchange):
        exchange_drain(*exchange)
    sib_drain(S["grads"], "gsib")
    sib_drain(S["toks"], "tsib")
    for d in range(Y):
        partner_copy(d).wait_send()
    for direction in range(2):
        for chunk in range(2):
            for h in range(hops(direction, chunk)):
                ring_copy(direction, chunk, h).wait_send()
    for copy in weights_out:
        copy.wait()


def per_device(
    queries,
    key_rows,
    value_rows,
    out_grad,
    expert_ids,
    gate_values,
    alibi_slope,
    expert_in,
    expert_out,
):
    E, N = lax.axis_size("seq"), lax.axis_size("exp")
    Y, Z = N // 2, WCH // 2
    BL = queries.shape[0]
    D, FL = expert_in.shape[1:]
    CAP = 5 * BL // (2 * E)
    scratch = scratch_table(E, Y, Z, BL, D, FL, CAP)
    vmem = pl.BlockSpec(memory_space=pltpu.VMEM)
    smem = pl.BlockSpec(memory_space=pltpu.SMEM)
    hbm = pl.BlockSpec(memory_space=pl.ANY)
    shape = jax.ShapeDtypeStruct
    return pl.pallas_call(
        functools.partial(body, list(scratch), E, Y, Z, CAP),
        out_shape=(
            shape(queries.shape, BF16),
            shape(queries.shape, BF16),
            shape(queries.shape, BF16),
            shape(expert_in.shape, BF16),
            shape(expert_out.shape, BF16),
        ),
        in_specs=[vmem] * 6 + [smem] + [hbm] * 2,
        out_specs=(vmem, vmem, vmem, hbm, hbm),
        scratch_shapes=list(scratch.values()),
        compiler_params=pltpu.CompilerParams(
            collective_id=0, has_side_effects=True, vmem_limit_bytes=56 * 2**20
        ),
    )(
        queries,
        key_rows,
        value_rows,
        out_grad,
        expert_ids.T,
        gate_values.T,
        alibi_slope,
        expert_in,
        expert_out,
    )


def solution(mesh):
    return jax.shard_map(
        per_device,
        mesh=mesh,
        in_specs=(
            P("seq", "exp"),
            P("seq", "exp"),
            P("seq", "exp"),
            P("seq", "exp"),
            P("seq", None),
            P("seq", None),
            P("exp"),
            P("seq", None, "exp"),
            P("seq", "exp", None),
        ),
        out_specs=(
            P("seq", "exp"),
            P("seq", "exp"),
            P("seq", "exp"),
            P("seq", None, "exp"),
            P("seq", "exp", None),
        ),
        check_vma=False,
    )
```

time: 590 us -> 147 us (0.25)
  waiting for transfers between devices: 279 us -> 0 us
  starting transfers between devices: 181 us -> 0 us
  Pallas kernels: 0 us -> 139 us
  matrix products: 35.4 us -> 0 us
  blocking collectives: 30.7 us -> 0 us
  other arithmetic: 21.3 us -> 0 us
  local copies, waits for them, and re-layouts: 21.9 us -> 6.32 us
  between operations: 14.7 us -> 1.3 us
    ppermute x64 -> x0, starting transfers between devices: 170 us -> none  [shifted(): return lax.ppermute(block, axis, route)]
    ppermute x64 -> x0, waiting for transfers between devices: 149 us -> none  [shifted(): return lax.ppermute(block, axis, route)]
    pallas_call x0 -> x1, Pallas kernels: none -> 139 us  [per_device(): pl.pallas_call(functools.partial(body, list(scratch), E, Y, Z, CAP), out_...]
    all_gather x2 -> x0, waiting for transfers between devices: 67.3 us -> none  [the longest x1 43.8 us: per_device(): full_grads = lax.all_gather(recv_grads, 'exp', axis=1, tiled=True)]
    unnamed x4 -> x0, waiting for transfers between devices: 57.7 us -> none
    dot_general x14 -> x0, matrix products: 35.4 us -> none  [the longest x1 5.78 us: window_scores(): jnp.einsum('ihd,jhd->hij', query_heads, key_stack, preferred_element_type...]
    all_to_all x2 -> x0, blocking collectives: 30.7 us -> none  [the longest x1 15.9 us: per_device(): lax.all_to_all(send_grads, 'seq', split_axis=0, concat_axis=0, tiled=True)]
    add x35 -> x0, other arithmetic: 16.2 us -> none  [the longest x16 14.7 us: relay_grads(): value_acc + lax.dynamic_index_in_dim(value_parts, index, 0, keepdims=False)]
  transfers between devices with their start and end apart: 68 -> 0, of which waited for: 64 -> 0; matrix products, arithmetic and copies ran while one was open for 5% -> 0% of each run, Pallas kernels for 0% -> 0%
where the time goes in v1:
time: 147 us
  Pallas kernels  139 us (95%)
  local copies, waits for them, and re-layouts  6.32 us (4%)
    pallas_call x1, Pallas kernels, per_device(): pl.pallas_call(functools.partial(body, list(scratch), E, Y, Z, CAP), out_...  139 us
    unnamed x11, local copies, waits for them, and re-layouts  6.32 us

profile of v1, /device:TPU:6, one launch (start us, length us, event | category | flops | bytes accessed | tf_op | source)
XLA Modules:
  0.0 146.6 jit_solution(17423476813282913378)
XLA Ops:
  1.3 139.0 %shard_map.128 = (bf16[256,128]{1,0:T(8,128)(2,1)}, bf16[256,128]{1,0:T(8,128)(2,1)}, bf16[256,128]{1,0:T(8,128)(2,1)}, bf16[1,2048,256]{2,1,0:T(8,128)(2,1)}, bf16[1,256,2048]{2,1,0:T(8,128)(2,1)}) custom-call(bf16[256,128]{1,0:T(8,128)(2,1)} %refs_0_.1, bf16[256,128]{1,0:T(8,128)(2,1)} %refs_1_.1, bf16[256,128]{1,0:T(8,128)(2,1)} %refs_2_.1, ...), custom_call_target="tpu_custom_call" | custom-call | tf_op jit(solution)/shard_map/pallas_call | solution.py:666
  140.3 0.0 copy-start.2
  140.3 1.5 %copy.20 = bf16[256,128]{1,0:T(8,128)(2,1)} copy(bf16[256,128]{1,0:T(8,128)(2,1)} %get-tuple-element.10) | data formatting | bytes 131072
  141.8 0.0 copy-done.2
  141.8 0.0 copy-start.1
  141.8 0.6 copy.21
  142.4 0.2 copy-done.1
  142.6 0.6 copy.22
  143.3 0.0 copy-start
  143.3 2.4 %copy.23 = bf16[1,2048,256]{2,1,0:T(8,128)(2,1)} copy(bf16[1,2048,256]{2,1,0:T(8,128)(2,1)} %get-tuple-element.13) | data formatting | bytes 2097152
  145.6 0.0 copy-done
  145.6 1.0 copy.24
Async XLA Ops:
  140.3 1.5 %copy-start.2 = (bf16[256,128]{1,0:T(8,128)(2,1)S(1)}, bf16[256,128]{1,0:T(8,128)(2,1)}, u32[]{:S(2)}) copy-start(bf16[256,128]{1,0:T(8,128)(2,1)} %get-tuple-element.11) | copy-start | bytes 196612
  141.8 0.9 copy-start.1
  143.3 2.4 %copy-start = (bf16[1,256,2048]{2,1,0:T(8,128)(2,1)S(1)}, bf16[1,256,2048]{2,1,0:T(8,128)(2,1)}, u32[]{:S(2)}) copy-start(bf16[1,256,2048]{2,1,0:T(8,128)(2,1)} %get-tuple-element.14) | copy-start | bytes 3145732

commit v2 on v1

--- a/solution.py
+++ b/solution.py
@@ -9,7 +9,7 @@
 
 HD = 128
 WCH = 16
-PAD = 32
+PAD = 24
 F32 = jnp.float32
 BF16 = jnp.bfloat16
 MESH = pl.DeviceIdType.MESH
@@ -44,8 +44,8 @@
 
 
 class GatherRing:
-    def __init__(self, count, me, device_of, view, sems, on_arrival=None):
-        self.n, self.me, self.view, self.on_arrival = count, me, view, on_arrival
+    def __init__(self, count, parts, me, device_of, view, sems, on_arrival=None):
+        self.n, self.parts, self.me, self.view, self.on_arrival = count, parts, me, view, on_arrival
         self.half = count // 2
         self.right = device_of(lax.rem(me + 1, count))
         self.left = device_of(lax.rem(me + count - 1, count))
@@ -55,11 +55,14 @@
         return lax.rem(self.me + (self.n - hops if direction == 0 else hops), self.n)
 
     def sends(self, direction, k, part):
-        return k < self.half - 1 or (k == self.half - 1 and part == direction)
+        return k < self.half - 1 or (k == self.half - 1 and self.ahead(direction, part))
+
+    def ahead(self, direction, part):
+        return (part < self.parts // 2) == (direction == 0)
 
     def copy(self, direction, k, part, hops):
         ref = self.view(self.block(direction, hops), part)
-        i = 2 * k + part
+        i = self.parts * k + part
         return remote(
             ref,
             ref,
@@ -68,14 +71,12 @@
             self.right if direction == 0 else self.left,
         )
 
-    def start(self):
-        for part in range(2):
-            for direction in range(2):
-                if self.sends(direction, 0, part):
-                    self.copy(direction, 0, part, 0).start()
+    def start(self, part):
+        for direction in range(2):
+            if self.sends(direction, 0, part):
+                self.copy(direction, 0, part, 0).start()
         if self.on_arrival:
-            for part in range(2):
-                self.on_arrival(self.me, 0, part)
+            self.on_arrival(self.me, 0, part)
 
     def step(self, k, part):
         for direction in range(2):
@@ -90,14 +91,14 @@
 
     def drain(self):
         for k in range(self.half):
-            for part in range(2):
+            for part in range(self.parts):
                 for direction in range(2):
                     if self.sends(direction, k, part):
                         self.copy(direction, k, part, k).wait_send()
 
 
 def scratch_table(E, Y, Z, BL, D, FL, CAP):
-    R, RP, hz, hy = E * CAP, E * PAD, max(Z // 2, 1), max(Y // 2, 1)
+    R, RP, hz, hy, X = E * CAP, E * PAD, max(Z // 2, 1), max(Y // 2, 1), E // Z
     table = dict(
         k3=((3, BL, HD), BF16),
         v3=((3, BL, HD), BF16),
@@ -108,14 +109,14 @@
         cb=((BL, BL), F32),
         osend=((Z, HD, BL), BF16),
         orecv=((Z, HD, BL), BF16),
-        lsend=((Z, 8, BL), F32),
-        lrecv=((Z, 8, BL), F32),
-        stats=((Z, 16, BL), F32),
+        lsend=((Z, 1, BL), F32),
+        lrecv=((Z, 1, BL), F32),
+        stats=((Z, 2, BL), F32),
         ot=((HD, BL), BF16),
         ogt=((HD, BL), F32),
         routing=((RP, 2 * BL), BF16),
-        comp=((R, RP), BF16),
-        compt=((RP, R), BF16),
+        comp=((R // X, RP // X), BF16),
+        compt=((RP // X, R // X), BF16),
         gs=((E, PAD, HD), BF16),
         gr=((E, PAD, HD), BF16),
         ts=((E, PAD, HD), BF16),
@@ -133,8 +134,8 @@
         pb=((Y, R, HD), BF16),
         sb=((Y, R, HD), BF16),
         rb=((Y, R, HD), BF16),
-        rs_stage=((2, 2 * hy, R // 2, HD), BF16),
-        rs_recv=((2, 2 * hy, R // 2, HD), BF16),
+        rs_stage=((2, X * hy, R // X, HD), BF16),
+        rs_recv=((2, X * hy, R // X, HD), BF16),
         dwi=((D, FL), BF16),
         dwo=((FL, D), BF16),
         dk3=((3, BL, HD), F32),
@@ -151,13 +152,14 @@
     counts = dict(
         kv_s=4, kv_r=4, o_s=Z, o_r=Z, l_s=Z, l_r=Z, st_s=Z, st_r=Z, dq_s=Z, dq_r=Z, dkv_s=4, dkv_r=4,
         ga_s=E, ga_r=E, ta_s=E, ta_r=E, ba_s=E, ba_r=E, w=2, dw=2,
-        gsib_s=2 * Y, gsib_r=2 * Y, tsib_s=2 * Y, tsib_r=2 * Y, psib_s=Y, psib_r=Y,
-    )
-    for ring, half in (("q", hz), ("g", hz), ("ygr", hy), ("ytk", hy), ("rs", hy)):
+        gsib_s=X * Y, gsib_r=X * Y, tsib_s=X * Y, tsib_r=X * Y, psib_s=Y, psib_r=Y,
+    )
+    for ring, half in (("q", 2 * hz), ("g", 2 * hz), ("ygr", X * hy), ("ytk", X * hy), ("rs", X * hy)):
         for end in ("_rs", "_rr", "_ls", "_lr"):
-            counts[ring + end] = 2 * half
+            counts[ring + end] = half
     for name, count in counts.items():
         shapes["sem_" + name] = pltpu.SemaphoreType.DMA((count,))
+    shapes["columns_in"] = pltpu.SemaphoreType.REGULAR
     return shapes
 
 
@@ -182,37 +184,31 @@
     def ydev(j):
         return (s, 2 * j + c)
 
+    drains = []
+    barrier = pltpu.get_barrier_semaphore()
+    near = [zdev(lax.rem(z + d, Z)) for d in range(1, Z)] + [xdev(x + d) for d in range(1, X)]
+    near += [ydev(lax.rem(y + 1, Y)), ydev(lax.rem(y + Y - 1, Y)), sibling]
+    for device in near:
+        pl.semaphore_signal(barrier, inc=1, device_id=device, device_id_type=MESH)
+
     weights_in = [
         pltpu.make_async_copy(win_ref.at[0], S["win"], S["sem_w"].at[0]),
         pltpu.make_async_copy(wout_ref.at[0], S["wout"], S["sem_w"].at[1]),
     ]
     for copy in weights_in:
         copy.start()
-
-    barrier = pltpu.get_barrier_semaphore()
-
-    def greet(i, carry):
-        pl.semaphore_signal(
-            barrier, inc=1, device_id=(lax.rem(s + i, E), e), device_id_type=MESH
-        )
-        return carry
-
-    lax.fori_loop(1, E, greet, 0)
-    for device in (ydev(lax.rem(y + 1, Y)), ydev(lax.rem(y + Y - 1, Y)), sibling):
-        pl.semaphore_signal(barrier, inc=1, device_id=device, device_id_type=MESH)
-
     S["qb"][z] = q_ref[...]
     S["k3"][0] = k_ref[...]
     S["v3"][0] = v_ref[...]
-    S["kt3"][0] = transposed(k_ref[...])
-    S["vt3"][0] = transposed(v_ref[...])
-    pl.semaphore_wait(barrier, E - 1 + 3)
+    pl.semaphore_wait(barrier, len(near))
 
     q_ring = GatherRing(
-        Z, z, zdev, lambda b, p: S["qb"].at[b, pl.ds(p * (BL // 2), BL // 2), :],
+        Z, 2, z, zdev, lambda b, p: S["qb"].at[b, pl.ds(p * (BL // 2), BL // 2), :],
         [S["sem_q_rs"], S["sem_q_rr"], S["sem_q_ls"], S["sem_q_lr"]],
     )
-    q_ring.start()
+    for part in range(2):
+        q_ring.start(part)
+    drains.append(q_ring.drain)
     kv_copies = []
     for hop in (1, 2):
         for which, (own, buf) in enumerate((("k3", "k3"), ("v3", "v3"))):
@@ -223,6 +219,12 @@
             )
             copy.start()
             kv_copies.append(copy)
+            drains.append(copy.wait_send)
+
+    for d in range(1, X):
+        pl.semaphore_signal(
+            S["columns_in"], inc=1, device_id=xdev(x + d), device_id_type=MESH
+        )
 
     flat = jnp.concatenate([ids_ref[0:1, :], ids_ref[1:2, :]], axis=1)
     hot = lax.broadcasted_iota(jnp.int32, (E, 2 * BL), 0) == flat
@@ -239,46 +241,76 @@
     ogt = jnp.transpose(og_ref[...].astype(F32))
     S["ogt"][...] = ogt
     scaled = jnp.concatenate([ogt * gates_ref[0:1, :], ogt * gates_ref[1:2, :]], axis=1)
-    S["gs"][...] = nt(S["routing"][...], scaled.astype(BF16)).astype(BF16).reshape(E, PAD, HD)
-
-    def exchange_start(send, recv, send_sem, recv_sem):
-        recv[s] = send[s]
-
-        def go(i, carry):
-            peer = lax.rem(s + i, E)
-            remote(send.at[peer], recv.at[s], send_sem.at[i], recv_sem.at[i], (peer, e)).start()
+    def spread(send, value):
+        send[...] = value.reshape(E, PAD, HD).astype(BF16)
+
+    def row_of(i):
+        return lax.rem(x + i, X)
+
+    def exchange_copy(exchange, i, j, outward):
+        send, recv, sems = exchange
+        k = i * Z + j
+        if outward:
+            peer = lax.rem(x + X - i, X) * Z + lax.rem(z + j, Z)
+            return remote(send.at[peer], recv.at[s], S[sems + "_s"].at[k], S[sems + "_r"].at[k], (peer, e))
+        peer = row_of(i) * Z + lax.rem(z + Z - j, Z)
+        return remote(send.at[peer], recv.at[peer], S[sems + "_s"].at[k], S[sems + "_r"].at[k], (peer, e))
+
+    def each_peer(i, act):
+        def go(j, carry):
+            act(j)
             return carry
 
-        lax.fori_loop(1, E, go, 0)
-
-    def exchange_wait(send, recv, send_sem, recv_sem):
-        def go(i, carry):
-            peer = lax.rem(s + E - i, E)
-            remote(send.at[peer], recv.at[peer], send_sem.at[i], recv_sem.at[i], (peer, e)).wait_recv()
-            return carry
-
-        lax.fori_loop(1, E, go, 0)
-
-    def exchange_drain(send, recv, send_sem, recv_sem):
-        def go(i, carry):
-            peer = lax.rem(s + i, E)
-            remote(send.at[peer], recv.at[s], send_sem.at[i], recv_sem.at[i], (peer, e)).wait_send()
-            return carry
-
-        lax.fori_loop(1, E, go, 0)
-
-    grad_exchange = (S["gs"], S["gr"], S["sem_ga_s"], S["sem_ga_r"])
-    token_exchange = (S["ts"], S["tr"], S["sem_ta_s"], S["sem_ta_r"])
-    back_exchange = (S["bs"], S["br"], S["sem_ba_s"], S["sem_ba_r"])
-    exchange_start(*grad_exchange)
-
-    padded = lax.broadcasted_iota(jnp.int32, (1, RP), 1)
-    packed_of = jnp.where(
-        (padded & (PAD - 1)) < CAP, (padded >> 5) * CAP + (padded & (PAD - 1)), -1
-    )
+        lax.fori_loop(1 if i == 0 else 0, Z, go, 0)
+
+    def exchange_send(exchange, i):
+        if i == 0:
+            exchange[1][s] = exchange[0][s]
+        each_peer(i, lambda j: exchange_copy(exchange, i, j, True).start())
+
+    def exchange_wait(exchange, i):
+        each_peer(i, lambda j: exchange_copy(exchange, i, j, False).wait_recv())
+
+    def exchange_drain(exchange):
+        for i in range(X):
+            each_peer(i, lambda j: exchange_copy(exchange, i, j, True).wait_send())
+
+    grad_exchange = (S["gs"], S["gr"], "sem_ga")
+    token_exchange = (S["ts"], S["tr"], "sem_ta")
+    back_exchange = (S["bs"], S["br"], "sem_ba")
+    spread(S["gs"], nt(S["routing"][...], scaled.astype(BF16)))
+    pl.semaphore_wait(S["columns_in"], X - 1)
+    for i in range(X):
+        exchange_send(grad_exchange, i)
+    drains.append(lambda: exchange_drain(grad_exchange))
+
+    per_part, padded_part = R // X, RP // X
+
+    def packed_of(index):
+        block = (index * (65536 // PAD + 1)) >> 16
+        inner = index - block * PAD
+        return jnp.where(inner < CAP, block * CAP + inner, -1)
+
     S["comp"][...] = jnp.where(
-        lax.broadcasted_iota(jnp.int32, (R, RP), 0) == packed_of, 1.0, 0.0
+        lax.broadcasted_iota(jnp.int32, (per_part, padded_part), 0)
+        == packed_of(lax.broadcasted_iota(jnp.int32, (per_part, padded_part), 1)),
+        1.0,
+        0.0,
     ).astype(BF16)
+    S["compt"][...] = jnp.where(
+        packed_of(lax.broadcasted_iota(jnp.int32, (padded_part, per_part), 0))
+        == lax.broadcasted_iota(jnp.int32, (padded_part, per_part), 1),
+        1.0,
+        0.0,
+    ).astype(BF16)
+
+    def part_rows(i):
+        align = 16 if per_part % 16 == 0 else 1
+        return pl.ds(pl.multiple_of(row_of(i) * per_part, align), per_part)
+
+    def pack(exchange, buf, i):
+        part = exchange[1][pl.ds(row_of(i) * Z, Z)].astype(F32).reshape(padded_part, HD)
+        buf[e, part_rows(i), :] = nn(S["comp"][...], part.astype(BF16)).astype(BF16)
 
     slope = slope_ref[0]
     S["cb"][...] = lax.broadcasted_iota(jnp.int32, (BL, BL), 0).astype(F32) * slope
@@ -315,7 +347,7 @@
             total = total + jnp.sum(p, axis=0, keepdims=True)
             out = out + nn(S["vt3"][r], p.astype(BF16))
         out = (out / total).astype(BF16)
-        log_norm = jnp.broadcast_to(top + jnp.log(total), (8, BL))
+        log_norm = top + jnp.log(total)
         if d == 0:
             S["orecv"][0] = out
             S["lrecv"][0] = log_norm
@@ -324,6 +356,8 @@
         S["lsend"][d] = log_norm
         out_copy(d).start()
         norm_copy(d).start()
+        drains.append(out_copy(d).wait_send)
+        drains.append(norm_copy(d).wait_send)
 
     def out_copy(d):
         return remote(S["osend"].at[d], S["orecv"].at[d], S["sem_o_s"].at[d], S["sem_o_r"].at[d],
@@ -333,55 +367,74 @@
         return remote(S["lsend"].at[d], S["lrecv"].at[d], S["sem_l_s"].at[d], S["sem_l_r"].at[d],
                       zdev(lax.rem(z + d, Z)))
 
-    for copy in kv_copies:
-        copy.wait_recv()
-    for r in (1, 2):
-        S["kt3"][r] = transposed(S["k3"][r])
-        S["vt3"][r] = transposed(S["v3"][r])
-    forward(0)
+    def feature_view(buf, block, core, part):
+        return buf.at[2 * block + core, part_rows(part), :]
 
     def feature_ring(buf, ring, sib):
         def arrived(block, distance, part):
-            sib_copy(buf, sib, block, distance, part).start()
+            sib_copy(buf, sib, block, distance, part, c).start()
 
         return GatherRing(
-            Y, y, ydev, lambda b, p: buf.at[2 * b + c, pl.ds(p * (R // 2), R // 2), :],
+            Y, X, y, ydev, lambda b, p: feature_view(buf, b, c, p),
             [S["sem_" + ring + end] for end in ("_rs", "_rr", "_ls", "_lr")], arrived,
         )
 
-    def sib_copy(buf, sib, block, distance, part):
-        ref = buf.at[2 * block + c, pl.ds(part * (R // 2), R // 2), :]
-        i = 2 * distance + part
+    def sib_copy(buf, sib, block, distance, part, core):
+        ref = feature_view(buf, block, core, part)
+        i = X * distance + part
         return remote(ref, ref, S["sem_" + sib + "_s"].at[i], S["sem_" + sib + "_r"].at[i], sibling)
 
     def sib_wait(buf, sib, distance):
-        block = lax.rem(y + distance, Y)
-        for part in range(2):
-            ref = buf.at[2 * block + 1 - c, pl.ds(part * (R // 2), R // 2), :]
-            i = 2 * distance + part
-            remote(ref, ref, S["sem_" + sib + "_s"].at[i], S["sem_" + sib + "_r"].at[i], sibling).wait_recv()
+        for part in range(X):
+            sib_copy(buf, sib, lax.rem(y + distance, Y), distance, part, 1 - c).wait_recv()
 
     def sib_drain(buf, sib):
         for distance in range(Y):
+            for part in range(X):
+                sib_copy(buf, sib, lax.rem(y + distance, Y), distance, part, c).wait_send()
+
+    def ring_from_exchange(exchange, buf, ring):
+        for i in range(X):
+            exchange_wait(exchange, i)
+            pack(exchange, buf, i)
+            ring.start(i)
+
+    grad_ring = feature_ring(S["grads"], "ygr", "gsib")
+    drains.append(grad_ring.drain)
+    drains.append(lambda: sib_drain(S["grads"], "gsib"))
+    y_half, z_half = Y // 2, Z // 2
+    grad_hops = list(range(y_half + 1))
+
+    def advance_grads():
+        if not grad_hops:
+            return
+        k = grad_hops.pop(0)
+        if k == 0:
+            ring_from_exchange(grad_exchange, S["grads"], grad_ring)
+        else:
+            for part in range(X):
+                grad_ring.step(k, part)
+
+    def neighbours(k, n):
+        return [0] if k == 0 else sorted({k, n - k})
+
+    for k in range(1, z_half + 2):
+        if k <= z_half:
             for part in range(2):
-                sib_copy(buf, sib, lax.rem(y + distance, Y), distance, part).wait_send()
-
-    exchange_wait(*grad_exchange)
-    S["grads"][e] = nn(S["comp"][...], S["gr"][...].reshape(RP, HD)).astype(BF16)
-    grad_ring = feature_ring(S["grads"], "ygr", "gsib")
-    grad_ring.start()
-    grad_steps = [(k, p) for k in range(1, Y // 2 + 1) for p in range(2)]
-
-    def advance_grads():
-        if grad_steps:
-            grad_ring.step(*grad_steps.pop(0))
-
-    for k in range(1, Z // 2 + 1):
-        for part in range(2):
-            q_ring.step(k, part)
-        for d in sorted({k, Z - k}):
+                q_ring.step(k, part)
+        if k == 1:
+            S["kt3"][0] = transposed(k_ref[...])
+            S["vt3"][0] = transposed(v_ref[...])
+            for copy in kv_copies:
+                copy.wait_recv()
+            for r in (1, 2):
+                S["kt3"][r] = transposed(S["k3"][r])
+                S["vt3"][r] = transposed(S["v3"][r])
+        for d in neighbours(k - 1, Z):
             forward(d)
-        advance_grads()
+        if k >= 2 and k <= z_half:
+            advance_grads()
+    advance_grads()
 
     for d in range(1, Z):
         out_copy(d).wait_recv()
@@ -396,14 +449,12 @@
     out_t = (merged / total).astype(BF16)
     S["ot"][...] = out_t
     log_norm = top + jnp.log(total)
-    S["stats"][z, 0:8, :] = jnp.broadcast_to(log_norm, (8, BL))
-
-    S["ts"][...] = (
-        nt(S["routing"][...], jnp.concatenate([out_t, out_t], axis=1))
-        .astype(BF16)
-        .reshape(E, PAD, HD)
-    )
-    exchange_start(*token_exchange)
+    S["stats"][z, 0:1, :] = log_norm
+
+    spread(S["ts"], nt(S["routing"][...], jnp.concatenate([out_t, out_t], axis=1)))
+    for i in range(X):
+        exchange_send(token_exchange, i)
+    drains.append(lambda: exchange_drain(token_exchange))
 
     def pair(buf, block):
         return jnp.concatenate([buf[2 * block], buf[2 * block + 1]], axis=1)
@@ -417,7 +468,7 @@
 
     for copy in weights_in:
         copy.wait()
-    while grad_steps:
+    while grad_hops:
         advance_grads()
     for n, d in enumerate(order):
         sib_wait(S["grads"], "gsib", d)
@@ -425,17 +476,10 @@
         term = nt(pair(S["grads"], block), S["wout"][:, columns(block)])
         S["thr"][...] = term if n == 0 else S["thr"][...] + term
 
-    exchange_wait(*token_exchange)
-    S["toks"][e] = nn(S["comp"][...], S["tr"][...].reshape(RP, HD)).astype(BF16)
     token_ring = feature_ring(S["toks"], "ytk", "tsib")
-    token_ring.start()
-    slots = lax.broadcasted_iota(jnp.int32, (RP, R), 0)
-    packed_rows = jnp.where(
-        (slots & (PAD - 1)) < CAP, (slots >> 5) * CAP + (slots & (PAD - 1)), -1
-    )
-    S["compt"][...] = jnp.where(
-        packed_rows == lax.broadcasted_iota(jnp.int32, (RP, R), 1), 1.0, 0.0
-    ).astype(BF16)
+    drains.append(token_ring.drain)
+    drains.append(lambda: sib_drain(S["toks"], "tsib"))
+    ring_from_exchange(token_exchange, S["toks"], token_ring)
 
     def pre_term(d):
         sib_wait(S["toks"], "tsib", d)
@@ -443,11 +487,11 @@
         term = nn(pair(S["toks"], block), S["win"][columns(block), :])
         S["pre"][...] = term if d == 0 else S["pre"][...] + term
 
-    pre_term(0)
-    for k in range(1, Y // 2 + 1):
-        for part in range(2):
-            token_ring.step(k, part)
-        for d in sorted({k, Y - k}):
+    for k in range(1, y_half + 2):
+        if k <= y_half:
+            for part in range(X):
+                token_ring.step(k, part)
+        for d in neighbours(k - 1, Y):
             pre_term(d)
 
     pre = S["pre"][...]
@@ -468,23 +512,26 @@
         S["pb"][block] = jnp.where(c == 0, first, second)
         S["sb"][block] = jnp.where(c == 0, second, first)
         partner_copy(d).start()
-
-    half = Y // 2
-    rows = R // 2
+        drains.append(partner_copy(d).wait_send)
+
+    half = y_half
 
     def hops(direction, chunk):
-        return half if direction == chunk else half - 1
+        return half if (chunk < X // 2) == (direction == 0) else half - 1
 
     def ring_copy(direction, chunk, h):
-        i = 2 * h + chunk
+        i = X * h + chunk
         ends = ("_rs", "_rr") if direction == 0 else ("_ls", "_lr")
         neighbour = ydev(lax.rem(y + 1, Y)) if direction == 0 else ydev(lax.rem(y + Y - 1, Y))
         return remote(S["rs_stage"].at[direction, i], S["rs_recv"].at[direction, i],
                       S["sem_rs" + ends[0]].at[i], S["sem_rs" + ends[1]].at[i], neighbour)
 
     def own_part(block, chunk):
-        span = pl.ds(chunk * rows, rows)
+        span = part_rows(chunk)
         return S["pb"][block, span, :].astype(F32) + S["rb"][block, span, :].astype(F32)
+
+    lanes = [(0, i) for i in range(X)] + [(1, (i + X // 2) % X) for i in range(X)]
+    lanes = [lane for both in zip(lanes[:X], lanes[X:]) for lane in both]
 
     weight_work = [("out", d) for d in order] + [("in", d) for d in order]
 
@@ -506,7 +553,7 @@
 
     per_hop = -(-2 * Y // half)
     for h in range(half):
-        for direction, chunk in ((0, 0), (1, 1), (0, 1), (1, 0)):
+        for direction, chunk in lanes:
             total_hops = hops(direction, chunk)
             if h >= total_hops:
                 continue
@@ -515,23 +562,23 @@
             value = own_part(lax.rem(y + distance, Y), chunk)
             if h > 0:
                 ring_copy(direction, chunk, h - 1).wait_recv()
-                value = value + S["rs_recv"][direction, 2 * (h - 1) + chunk].astype(F32)
-            S["rs_stage"][direction, 2 * h + chunk] = value.astype(BF16)
+                value = value + S["rs_recv"][direction, X * (h - 1) + chunk].astype(F32)
+            S["rs_stage"][direction, X * h + chunk] = value.astype(BF16)
             ring_copy(direction, chunk, h).start()
+            drains.append(ring_copy(direction, chunk, h).wait_send)
         some_weight_work(per_hop)
     need_partner(0)
-    sums = []
-    for chunk in range(2):
+    for chunk in range(X):
         value = own_part(y, chunk)
         for direction in range(2):
             last = hops(direction, chunk) - 1
             if last >= 0:
                 ring_copy(direction, chunk, last).wait_recv()
-                value = value + S["rs_recv"][direction, 2 * last + chunk].astype(F32)
-        sums.append(value.astype(BF16))
-    back = jnp.concatenate(sums, axis=0)
-    S["bs"][...] = nn(S["compt"][...], back).astype(BF16).reshape(E, PAD, HD)
-    exchange_start(*back_exchange)
+                value = value + S["rs_recv"][direction, X * last + chunk].astype(F32)
+        padded = nn(S["compt"][...], value.astype(BF16)).reshape(Z, PAD, HD)
+        S["bs"][pl.ds(row_of(chunk) * Z, Z)] = padded.astype(BF16)
+        exchange_send(back_exchange, (X - chunk) % X)
+    drains.append(lambda: exchange_drain(back_exchange))
     some_weight_work(2 * Y)
     weights_out = [
         pltpu.make_async_copy(S["dwi"], dwi_ref.at[0], S["sem_dw"].at[0]),
@@ -539,15 +586,18 @@
     ]
     for copy in weights_out:
         copy.start()
-    exchange_wait(*back_exchange)
-    combined = tn(S["br"][...].reshape(RP, HD), S["routing"][...])
+        drains.append(copy.wait)
+    for i in range(X):
+        exchange_wait(back_exchange, i)
+    returned = S["br"][...].astype(F32).reshape(RP, HD).astype(BF16)
+    combined = tn(returned, S["routing"][...])
     grad_t = (S["ogt"][...] + combined[:, :BL] + combined[:, BL:]).astype(BF16).astype(F32)
     delta = jnp.sum(grad_t * S["ot"][...].astype(F32), axis=0, keepdims=True)
-    S["stats"][z, 8:16, :] = jnp.broadcast_to(delta, (8, BL))
+    S["stats"][z, 1:2, :] = delta
     S["gb"][z] = jnp.transpose(grad_t).astype(BF16)
 
     g_ring = GatherRing(
-        Z, z, zdev, lambda b, p: S["gb"].at[b, pl.ds(p * (BL // 2), BL // 2), :],
+        Z, 2, z, zdev, lambda b, p: S["gb"].at[b, pl.ds(p * (BL // 2), BL // 2), :],
         [S["sem_g_rs"], S["sem_g_rr"], S["sem_g_ls"], S["sem_g_lr"]],
     )
 
@@ -555,9 +605,12 @@
         ref = S["stats"].at[block]
         return remote(ref, ref, S["sem_st_s"].at[d], S["sem_st_r"].at[d], zdev(lax.rem(z + d, Z)))
 
+    for part in range(2):
+        g_ring.start(part)
+    drains.append(g_ring.drain)
     for d in range(1, Z):
         stats_copy(d, z).start()
-    g_ring.start()
+        drains.append(stats_copy(d, z).wait_send)
 
     def dq_copy(d):
         return remote(S["dqsend"].at[d], S["dqrecv"].at[d], S["sem_dq_s"].at[d], S["sem_dq_r"].at[d],
@@ -566,7 +619,7 @@
     def backward(d):
         j = lax.rem(z + d, Z)
         queries, grads = S["qb"][j], S["gb"][j]
-        norm, dlt = S["stats"][j, 0:1, :], S["stats"][j, 8:9, :]
+        norm, dlt = S["stats"][j, 0:1, :], S["stats"][j, 1:2, :]
         dq = 0.0
         for r, offset, mask in pieces(d, j):
             p = jnp.exp(scores_of(r, offset, mask, queries) - norm)
@@ -585,13 +638,15 @@
         else:
             S["dqsend"][d] = dq.astype(BF16)
             dq_copy(d).start()
-
-    backward(0)
-    for k in range(1, Z // 2 + 1):
-        for part in range(2):
-            g_ring.step(k, part)
-        for d in sorted({k, Z - k}):
-            stats_copy(Z - d, lax.rem(z + d, Z)).wait_recv()
+            drains.append(dq_copy(d).wait_send)
+
+    for k in range(1, z_half + 2):
+        if k <= z_half:
+            for part in range(2):
+                g_ring.step(k, part)
+        for d in neighbours(k - 1, Z):
+            if d:
+                stats_copy(Z - d, lax.rem(z + d, Z)).wait_recv()
             backward(d)
 
     dkv_copies = []
@@ -604,6 +659,7 @@
                           S["sem_dkv_s"].at[i], S["sem_dkv_r"].at[i], xdev(x + X - hop))
             copy.start()
             dkv_copies.append(copy)
+            drains.append(copy.wait_send)
 
     dq = S["dqown"][...]
     for d in range(1, Z):
@@ -619,26 +675,16 @@
         S["dv3"][0] + S["dvrecv"][0].astype(F32) + S["dvrecv"][1].astype(F32)
     ).astype(BF16)
 
-    for copy in kv_copies + dkv_copies:
-        copy.wait_send()
-    for ring in (q_ring, g_ring, grad_ring, token_ring):
-        ring.drain()
-    for d in range(1, Z):
-        out_copy(d).wait_send()
-        norm_copy(d).wait_send()
-        stats_copy(d, z).wait_send()
-        dq_copy(d).wait_send()
-    for exchange in (grad_exchange, token_exchange, back_exchange):
-        exchange_drain(*exchange)
-    sib_drain(S["grads"], "gsib")
-    sib_drain(S["toks"], "tsib")
-    for d in range(Y):
-        partner_copy(d).wait_send()
-    for direction in range(2):
-        for chunk in range(2):
-            for h in range(hops(direction, chunk)):
-                ring_copy(direction, chunk, h).wait_send()
-    for copy in weights_out:
+    for f in drains:
+        f()
+
+
+def hand_over(*refs):
+    sems = refs[10]
+    copies = [pltpu.make_async_copy(refs[i], refs[5 + i], sems.at[i]) for i in range(5)]
+    for copy in copies:
+        copy.start()
+    for copy in copies:
         copy.wait()
 
 
@@ -663,7 +709,7 @@
     smem = pl.BlockSpec(memory_space=pltpu.SMEM)
     hbm = pl.BlockSpec(memory_space=pl.ANY)
     shape = jax.ShapeDtypeStruct
-    return pl.pallas_call(
+    outs = pl.pallas_call(
         functools.partial(body, list(scratch), E, Y, Z, CAP),
         out_shape=(
             shape(queries.shape, BF16),
@@ -689,6 +735,13 @@
         expert_in,
         expert_out,
     )
+    return pl.pallas_call(
+        hand_over,
+        out_shape=tuple(shape(out.shape, out.dtype) for out in outs),
+        in_specs=[hbm] * 5,
+        out_specs=(hbm,) * 5,
+        scratch_shapes=[pltpu.SemaphoreType.DMA((5,))],
+    )(*outs)
 
 
 def solution(mesh):

time: 147 us -> 198 us (1.35)
  Pallas kernels: 139 us -> 195 us
  local copies, waits for them, and re-layouts: 6.32 us -> 0 us
    pallas_call x0 -> x1, Pallas kernels: none -> 70.6 us  [per_device(): pl.pallas_call(hand_over, out_shape=tuple((shape(out.shape, out.dtype) fo...]
    pallas_call x1, Pallas kernels: 139 us -> 125 us  [per_device(): pl.pallas_call(functools.partial(body, list(scratch), E, Y, Z, CAP), out_...]
    unnamed x11 -> x0, local copies, waits for them, and re-layouts: 6.32 us -> none
where the time goes in v2:
time: 198 us; the launch traced here: 197 us
  Pallas kernels  195 us (98%)
    pallas_call x1, Pallas kernels, per_device(): pl.pallas_call(functools.partial(body, list(scratch), E, Y, Z, CAP), out_...  125 us
    pallas_call x1, Pallas kernels, per_device(): pl.pallas_call(hand_over, out_shape=tuple((shape(out.shape, out.dtype) fo...  70.6 us

profile of v2, /device:TPU:6, one launch (start us, length us, event | category | flops | bytes accessed | tf_op | source)
XLA Modules:
  0.0 196.8 jit_solution(5888987654126164630)
XLA Ops:
  1.3 124.7 %shard_map.128 = (bf16[256,128]{1,0:T(8,128)(2,1)}, bf16[256,128]{1,0:T(8,128)(2,1)}, bf16[256,128]{1,0:T(8,128)(2,1)}, bf16[1,2048,256]{2,1,0:T(8,128)(2,1)}, bf16[1,256,2048]{2,1,0:T(8,128)(2,1)}) custom-call(bf16[256,128]{1,0:T(8,128)(2,1)} %refs_0_.1, bf16[256,128]{1,0:T(8,128)(2,1)} %refs_1_.1, bf16[256,128]{1,0:T(8,128)(2,1)} %refs_2_.1, ...), custom_call_target="tpu_custom_call" | custom-call | tf_op jit(solution)/shard_map/pallas_call | solution.py:712
  126.0 70.6 %shard_map.129 = (bf16[256,128]{1,0:T(8,128)(2,1)}, bf16[256,128]{1,0:T(8,128)(2,1)}, bf16[256,128]{1,0:T(8,128)(2,1)}, bf16[1,2048,256]{2,1,0:T(8,128)(2,1)}, bf16[1,256,2048]{2,1,0:T(8,128)(2,1)}) custom-call(bf16[256,128]{1,0:T(8,128)(2,1)} %get-tuple-element.10.refs_0_, bf16[256,128]{1,0:T(8,128)(2,1)} %get-tuple-element.11.refs_1_, ...), custom_call_target="tpu_custom_call" | custom-call | tf_op jit(solution)/shard_map/pallas_call | solution.py:738

commit v3 on v2

--- a/solution.py
+++ b/solution.py
@@ -44,8 +44,8 @@
 
 
 class GatherRing:
-    def __init__(self, count, parts, me, device_of, view, sems, on_arrival=None):
-        self.n, self.parts, self.me, self.view, self.on_arrival = count, parts, me, view, on_arrival
+    def __init__(self, count, parts, me, device_of, view, sems):
+        self.n, self.parts, self.me, self.view = count, parts, me, view
         self.half = count // 2
         self.right = device_of(lax.rem(me + 1, count))
         self.left = device_of(lax.rem(me + count - 1, count))
@@ -75,8 +75,6 @@
         for direction in range(2):
             if self.sends(direction, 0, part):
                 self.copy(direction, 0, part, 0).start()
-        if self.on_arrival:
-            self.on_arrival(self.me, 0, part)
 
     def step(self, k, part):
         for direction in range(2):
@@ -85,9 +83,6 @@
             self.copy(direction, k - 1, part, k).wait_recv()
             if self.sends(direction, k, part):
                 self.copy(direction, k, part, k).start()
-            if self.on_arrival:
-                distance = (self.n - k if direction == 0 else k) % self.n
-                self.on_arrival(self.block(direction, k), distance, part)
 
     def drain(self):
         for k in range(self.half):
@@ -136,8 +131,6 @@
         rb=((Y, R, HD), BF16),
         rs_stage=((2, X * hy, R // X, HD), BF16),
         rs_recv=((2, X * hy, R // X, HD), BF16),
-        dwi=((D, FL), BF16),
-        dwo=((FL, D), BF16),
         dk3=((3, BL, HD), F32),
         dv3=((3, BL, HD), F32),
         dksend=((2, BL, HD), BF16),
@@ -151,7 +144,7 @@
     shapes = {name: pltpu.VMEM(shape, dtype) for name, (shape, dtype) in table.items()}
     counts = dict(
         kv_s=4, kv_r=4, o_s=Z, o_r=Z, l_s=Z, l_r=Z, st_s=Z, st_r=Z, dq_s=Z, dq_r=Z, dkv_s=4, dkv_r=4,
-        ga_s=E, ga_r=E, ta_s=E, ta_r=E, ba_s=E, ba_r=E, w=2, dw=2,
+        ga_s=E, ga_r=E, ta_s=E, ta_r=E, ba_s=E, ba_r=E, w=2,
         gsib_s=X * Y, gsib_r=X * Y, tsib_s=X * Y, tsib_r=X * Y, psib_s=Y, psib_r=Y,
     )
     for ring, half in (("q", 2 * hz), ("g", 2 * hz), ("ygr", X * hy), ("ytk", X * hy), ("rs", X * hy)):
@@ -221,6 +214,15 @@
             kv_copies.append(copy)
             drains.append(copy.wait_send)
 
+    y_half, z_half = Y // 2, Z // 2
+    query_hops = list(range(1, z_half + 1))
+
+    def take_queries(upto):
+        while query_hops and query_hops[0] <= upto:
+            k = query_hops.pop(0)
+            for part in range(2):
+                q_ring.step(k, part)
+
     for d in range(1, X):
         pl.semaphore_signal(
             S["columns_in"], inc=1, device_id=xdev(x + d), device_id_type=MESH
@@ -279,10 +281,12 @@
     token_exchange = (S["ts"], S["tr"], "sem_ta")
     back_exchange = (S["bs"], S["br"], "sem_ba")
     spread(S["gs"], nt(S["routing"][...], scaled.astype(BF16)))
+    take_queries(1)
     pl.semaphore_wait(S["columns_in"], X - 1)
     for i in range(X):
         exchange_send(grad_exchange, i)
     drains.append(lambda: exchange_drain(grad_exchange))
+    take_queries(2)
 
     per_part, padded_part = R // X, RP // X
 
@@ -370,39 +374,58 @@
     def feature_view(buf, block, core, part):
         return buf.at[2 * block + core, part_rows(part), :]
 
-    def feature_ring(buf, ring, sib):
-        def arrived(block, distance, part):
-            sib_copy(buf, sib, block, distance, part, c).start()
-
+    def feature_ring(buf, ring):
         return GatherRing(
             Y, X, y, ydev, lambda b, p: feature_view(buf, b, c, p),
-            [S["sem_" + ring + end] for end in ("_rs", "_rr", "_ls", "_lr")], arrived,
+            [S["sem_" + ring + end] for end in ("_rs", "_rr", "_ls", "_lr")],
         )
 
-    def sib_copy(buf, sib, block, distance, part, core):
-        ref = feature_view(buf, block, core, part)
-        i = X * distance + part
-        return remote(ref, ref, S["sem_" + sib + "_s"].at[i], S["sem_" + sib + "_r"].at[i], sibling)
+    def sib_copies(buf, sib, distance, core):
+        block = 2 * lax.rem(y + distance, Y) + core
+        refs = [buf.at[block]]
+        if distance == y_half:
+            refs = [buf.at[block, part_rows(part), :] for part in range(X)]
+        return [
+            remote(ref, ref, S["sem_" + sib + "_s"].at[distance + Y * n],
+                   S["sem_" + sib + "_r"].at[distance + Y * n], sibling)
+            for n, ref in enumerate(refs)
+        ]
+
+    def sib_send(buf, sib, k):
+        for distance in neighbours(k, Y):
+            for copy in sib_copies(buf, sib, distance, c):
+                copy.start()
 
     def sib_wait(buf, sib, distance):
-        for part in range(X):
-            sib_copy(buf, sib, lax.rem(y + distance, Y), distance, part, 1 - c).wait_recv()
+        for copy in sib_copies(buf, sib, distance, 1 - c):
+            copy.wait_recv()
 
     def sib_drain(buf, sib):
         for distance in range(Y):
-            for part in range(X):
-                sib_copy(buf, sib, lax.rem(y + distance, Y), distance, part, c).wait_send()
-
-    def ring_from_exchange(exchange, buf, ring):
+            for copy in sib_copies(buf, sib, distance, c):
+                copy.wait_send()
+
+    def ring_hop(ring, buf, sib, k):
+        for part in range(X):
+            ring.step(k, part)
+            if k == y_half:
+                sib_copies(buf, sib, k, c)[part].start()
+        if k < y_half:
+            sib_send(buf, sib, k)
+
+    def neighbours(k, n):
+        return [0] if k == 0 else sorted({k, n - k})
+
+    def ring_from_exchange(exchange, buf, ring, sib):
         for i in range(X):
             exchange_wait(exchange, i)
             pack(exchange, buf, i)
             ring.start(i)
-
-    grad_ring = feature_ring(S["grads"], "ygr", "gsib")
+        sib_send(buf, sib, 0)
+
+    grad_ring = feature_ring(S["grads"], "ygr")
     drains.append(grad_ring.drain)
     drains.append(lambda: sib_drain(S["grads"], "gsib"))
-    y_half, z_half = Y // 2, Z // 2
     grad_hops = list(range(y_half + 1))
 
     def advance_grads():
@@ -410,31 +433,26 @@
             return
         k = grad_hops.pop(0)
         if k == 0:
-            ring_from_exchange(grad_exchange, S["grads"], grad_ring)
+            ring_from_exchange(grad_exchange, S["grads"], grad_ring, "gsib")
         else:
-            for part in range(X):
-                grad_ring.step(k, part)
-
-    def neighbours(k, n):
-        return [0] if k == 0 else sorted({k, n - k})
-
-    for k in range(1, z_half + 2):
-        if k <= z_half:
-            for part in range(2):
-                q_ring.step(k, part)
-        if k == 1:
-            S["kt3"][0] = transposed(k_ref[...])
-            S["vt3"][0] = transposed(v_ref[...])
-            for copy in kv_copies:
-                copy.wait_recv()
-            for r in (1, 2):
-                S["kt3"][r] = transposed(S["k3"][r])
-                S["vt3"][r] = transposed(S["v3"][r])
-        for d in neighbours(k - 1, Z):
+            ring_hop(grad_ring, S["grads"], "gsib", k)
+
+    S["kt3"][0] = transposed(k_ref[...])
+    S["vt3"][0] = transposed(v_ref[...])
+    for copy in kv_copies:
+        copy.wait_recv()
+    for r in (1, 2):
+        S["kt3"][r] = transposed(S["k3"][r])
+        S["vt3"][r] = transposed(S["v3"][r])
+    forward(0)
+    take_queries(3)
+    for k in range(1, z_half + 1):
+        if k == z_half:
+            take_queries(k)
+        for d in neighbours(k, Z):
             forward(d)
-        if k >= 2 and k <= z_half:
+        if k != 2:
             advance_grads()
-    advance_grads()
 
     for d in range(1, Z):
         out_copy(d).wait_recv()
@@ -454,6 +472,8 @@
     spread(S["ts"], nt(S["routing"][...], jnp.concatenate([out_t, out_t], axis=1)))
     for i in range(X):
         exchange_send(token_exchange, i)
+        if i == X // 2 - 1:
+            advance_grads()
     drains.append(lambda: exchange_drain(token_exchange))
 
     def pair(buf, block):
@@ -476,10 +496,10 @@
         term = nt(pair(S["grads"], block), S["wout"][:, columns(block)])
         S["thr"][...] = term if n == 0 else S["thr"][...] + term
 
-    token_ring = feature_ring(S["toks"], "ytk", "tsib")
+    token_ring = feature_ring(S["toks"], "ytk")
     drains.append(token_ring.drain)
     drains.append(lambda: sib_drain(S["toks"], "tsib"))
-    ring_from_exchange(token_exchange, S["toks"], token_ring)
+    ring_from_exchange(token_exchange, S["toks"], token_ring, "tsib")
 
     def pre_term(d):
         sib_wait(S["toks"], "tsib", d)
@@ -489,14 +509,12 @@
 
     for k in range(1, y_half + 2):
         if k <= y_half:
-            for part in range(X):
-                token_ring.step(k, part)
+            ring_hop(token_ring, S["toks"], "tsib", k)
         for d in neighbours(k - 1, Y):
             pre_term(d)
 
     pre = S["pre"][...]
     logistic = 1.0 / (1.0 + jnp.exp(-pre))
-    S["hid"][...] = jnp.transpose(pre * logistic).astype(BF16)
     S["hg"][...] = (S["thr"][...] * logistic * (1.0 + pre * (1.0 - logistic))).astype(BF16)
 
     def partner_copy(distance):
@@ -514,6 +532,7 @@
         partner_copy(d).start()
         drains.append(partner_copy(d).wait_send)
 
+    S["hid"][...] = jnp.transpose(pre * logistic).astype(BF16)
     half = y_half
 
     def hops(direction, chunk):
@@ -540,9 +559,9 @@
             which, d = weight_work.pop(0)
             block = lax.rem(y + d, Y)
             if which == "out":
-                S["dwo"][:, columns(block)] = nn(S["hid"][...], pair(S["grads"], block)).astype(BF16)
+                dwo_ref[0, :, columns(block)] = nn(S["hid"][...], pair(S["grads"], block)).astype(BF16)
             else:
-                S["dwi"][columns(block), :] = tn(pair(S["toks"], block), S["hg"][...]).astype(BF16)
+                dwi_ref[0, columns(block), :] = tn(pair(S["toks"], block), S["hg"][...]).astype(BF16)
 
     waited = set()
 
@@ -580,13 +599,6 @@
         exchange_send(back_exchange, (X - chunk) % X)
     drains.append(lambda: exchange_drain(back_exchange))
     some_weight_work(2 * Y)
-    weights_out = [
-        pltpu.make_async_copy(S["dwi"], dwi_ref.at[0], S["sem_dw"].at[0]),
-        pltpu.make_async_copy(S["dwo"], dwo_ref.at[0], S["sem_dw"].at[1]),
-    ]
-    for copy in weights_out:
-        copy.start()
-        drains.append(copy.wait)
     for i in range(X):
         exchange_wait(back_exchange, i)
     returned = S["br"][...].astype(F32).reshape(RP, HD).astype(BF16)
@@ -708,18 +720,12 @@
     vmem = pl.BlockSpec(memory_space=pltpu.VMEM)
     smem = pl.BlockSpec(memory_space=pltpu.SMEM)
     hbm = pl.BlockSpec(memory_space=pl.ANY)
-    shape = jax.ShapeDtypeStruct
+    kept = [queries.shape] * 3 + [expert_in.shape, expert_out.shape]
     outs = pl.pallas_call(
         functools.partial(body, list(scratch), E, Y, Z, CAP),
-        out_shape=(
-            shape(queries.shape, BF16),
-            shape(queries.shape, BF16),
-            shape(queries.shape, BF16),
-            shape(expert_in.shape, BF16),
-            shape(expert_out.shape, BF16),
-        ),
+        out_shape=tuple(pltpu.VMEM(out, BF16) for out in kept),
         in_specs=[vmem] * 6 + [smem] + [hbm] * 2,
-        out_specs=(vmem, vmem, vmem, hbm, hbm),
+        out_specs=(vmem,) * 5,
         scratch_shapes=list(scratch.values()),
         compiler_params=pltpu.CompilerParams(
             collective_id=0, has_side_effects=True, vmem_limit_bytes=56 * 2**20
@@ -737,11 +743,11 @@
     )
     return pl.pallas_call(
         hand_over,
-        out_shape=tuple(shape(out.shape, out.dtype) for out in outs),
-        in_specs=[hbm] * 5,
+        out_shape=tuple(jax.ShapeDtypeStruct(out, BF16) for out in kept),
+        in_specs=[vmem] * 5,
         out_specs=(hbm,) * 5,
         scratch_shapes=[pltpu.SemaphoreType.DMA((5,))],
-    )(*outs)
+    )(*(pltpu.with_memory_space_constraint(out, pltpu.VMEM) for out in outs))
 
 
 def solution(mesh):

time: 198 us -> 127 us (0.64)
  Pallas kernels: 195 us -> 125 us
    pallas_call x1, Pallas kernels: 70.6 us -> 1.43 us  [per_device(): pl.pallas_call(hand_over, out_shape=tuple((jax.ShapeDtypeStruct(out, BF16...]
where the time goes in v3:
time: 127 us; the launch traced here: 126 us
  Pallas kernels  125 us (98%)
  between operations  1.45 us (1%)
    pallas_call x1, Pallas kernels, per_device(): pl.pallas_call(functools.partial(body, list(scratch), E, Y, Z, CAP), out_...  123 us

profile of v3, /device:TPU:6, one launch (start us, length us, event | category | flops | bytes accessed | tf_op | source)
XLA Modules:
  0.0 126.3 jit_solution(14034372561838213475)
XLA Ops:
  1.3 123.4 %shard_map.128 = (bf16[256,128]{1,0:T(8,128)(2,1)S(1)}, bf16[256,128]{1,0:T(8,128)(2,1)S(1)}, bf16[256,128]{1,0:T(8,128)(2,1)S(1)}, bf16[1,2048,256]{2,1,0:T(8,128)(2,1)S(1)}, bf16[1,256,2048]{2,1,0:T(8,128)(2,1)S(1)}) custom-call(bf16[256,128]{1,0:T(8,128)(2,1)} %refs_0_.1, bf16[256,128]{1,0:T(8,128)(2,1)} %refs_1_.1, bf16[256,128]{1,0:T(8,128)(2,1)} %refs_2_.1, ...), custom_call_target="tpu_custom_call" | custom-call | tf_op jit(solution)/shard_map/pallas_call | solution.py:724
  124.7 1.4 %shard_map.129 = (bf16[256,128]{1,0:T(8,128)(2,1)}, bf16[256,128]{1,0:T(8,128)(2,1)}, bf16[256,128]{1,0:T(8,128)(2,1)}, bf16[1,2048,256]{2,1,0:T(8,128)(2,1)}, bf16[1,256,2048]{2,1,0:T(8,128)(2,1)}) custom-call(bf16[256,128]{1,0:T(8,128)(2,1)S(1)} %get-tuple-element.10.refs_0_, bf16[256,128]{1,0:T(8,128)(2,1)S(1)} %get-tuple-element.11.refs_1_, ...), custom_call_target="tpu_custom_call" | custom-call | tf_op jit(solution)/shard_map/pallas_call | solution.py:744

commit v4 on v3

--- a/solution.py
+++ b/solution.py
@@ -100,6 +100,7 @@
         kt3=((3, HD, BL), BF16),
         vt3=((3, HD, BL), BF16),
         qb=((Z, BL, HD), BF16),
+        relay=((BL, HD), BF16),
         gb=((Z, BL, HD), BF16),
         cb=((BL, BL), F32),
         osend=((Z, HD, BL), BF16),
@@ -144,7 +145,7 @@
     shapes = {name: pltpu.VMEM(shape, dtype) for name, (shape, dtype) in table.items()}
     counts = dict(
         kv_s=4, kv_r=4, o_s=Z, o_r=Z, l_s=Z, l_r=Z, st_s=Z, st_r=Z, dq_s=Z, dq_r=Z, dkv_s=4, dkv_r=4,
-        ga_s=E, ga_r=E, ta_s=E, ta_r=E, ba_s=E, ba_r=E, w=2,
+        ga_s=E, ga_r=E, ta_s=E, ta_r=E, ba_s=E, ba_r=E, w=2, own=3, re_s=2, re_r=2,
         gsib_s=X * Y, gsib_r=X * Y, tsib_s=X * Y, tsib_r=X * Y, psib_s=Y, psib_r=Y,
     )
     for ring, half in (("q", 2 * hz), ("g", 2 * hz), ("ygr", X * hy), ("ytk", X * hy), ("rs", X * hy)):
@@ -184,15 +185,21 @@
     for device in near:
         pl.semaphore_signal(barrier, inc=1, device_id=device, device_id_type=MESH)
 
+    own_rows = [
+        pltpu.make_async_copy(q_ref, S["qb"].at[z], S["sem_own"].at[0]),
+        pltpu.make_async_copy(k_ref, S["k3"].at[0], S["sem_own"].at[1]),
+        pltpu.make_async_copy(v_ref, S["v3"].at[0], S["sem_own"].at[2]),
+    ]
+    for copy in own_rows:
+        copy.start()
     weights_in = [
         pltpu.make_async_copy(win_ref.at[0], S["win"], S["sem_w"].at[0]),
         pltpu.make_async_copy(wout_ref.at[0], S["wout"], S["sem_w"].at[1]),
     ]
     for copy in weights_in:
         copy.start()
-    S["qb"][z] = q_ref[...]
-    S["k3"][0] = k_ref[...]
-    S["v3"][0] = v_ref[...]
+    for copy in own_rows:
+        copy.wait()
     pl.semaphore_wait(barrier, len(near))
 
     q_ring = GatherRing(
@@ -206,6 +213,8 @@
     for hop in (1, 2):
         for which, (own, buf) in enumerate((("k3", "k3"), ("v3", "v3"))):
             i = 2 * (hop - 1) + which
+            if i == 3 and X == 4:
+                continue
             copy = remote(
                 S[own].at[0], S[buf].at[hop], S["sem_kv_s"].at[i], S["sem_kv_r"].at[i],
                 xdev(x + hop),
@@ -213,6 +222,16 @@
             copy.start()
             kv_copies.append(copy)
             drains.append(copy.wait_send)
+
+    def relay_copy(leg):
+        return remote(
+            S["v3"].at[0] if leg == 0 else S["relay"],
+            S["relay"] if leg == 0 else S["v3"].at[2],
+            S["sem_re_s"].at[leg], S["sem_re_r"].at[leg], xdev(x + X - 1),
+        )
+
+    if X == 4:
+        relay_copy(0).start()
 
     y_half, z_half = Y // 2, Z // 2
     query_hops = list(range(1, z_half + 1))
@@ -282,6 +301,10 @@
     back_exchange = (S["bs"], S["br"], "sem_ba")
     spread(S["gs"], nt(S["routing"][...], scaled.astype(BF16)))
     take_queries(1)
+    if X == 4:
+        relay_copy(0).wait_recv()
+        relay_copy(1).start()
+        drains += [relay_copy(0).wait_send, relay_copy(1).wait_send]
     pl.semaphore_wait(S["columns_in"], X - 1)
     for i in range(X):
         exchange_send(grad_exchange, i)
@@ -437,10 +460,12 @@
         else:
             ring_hop(grad_ring, S["grads"], "gsib", k)
 
-    S["kt3"][0] = transposed(k_ref[...])
-    S["vt3"][0] = transposed(v_ref[...])
+    S["kt3"][0] = transposed(S["k3"][0])
+    S["vt3"][0] = transposed(S["v3"][0])
     for copy in kv_copies:
         copy.wait_recv()
+    if X == 4:
+        relay_copy(1).wait_recv()
     for r in (1, 2):
         S["kt3"][r] = transposed(S["k3"][r])
         S["vt3"][r] = transposed(S["v3"][r])
@@ -724,7 +749,7 @@
     outs = pl.pallas_call(
         functools.partial(body, list(scratch), E, Y, Z, CAP),
         out_shape=tuple(pltpu.VMEM(out, BF16) for out in kept),
-        in_specs=[vmem] * 6 + [smem] + [hbm] * 2,
+        in_specs=[hbm] * 3 + [vmem] * 3 + [smem] + [hbm] * 2,
         out_specs=(vmem,) * 5,
         scratch_shapes=list(scratch.values()),
         compiler_params=pltpu.CompilerParams(

time: 127 us -> 128 us (level)
  no operation moved by 1% of the time
where the time goes in v4:
time: 128 us; the launch traced here: 126 us
  Pallas kernels  125 us (98%)
  between operations  1.45 us (1%)
    pallas_call x1, Pallas kernels, per_device(): pl.pallas_call(functools.partial(body, list(scratch), E, Y, Z, CAP), out_...  123 us

profile of v4, /device:TPU:6, one launch (start us, length us, event | category | flops | bytes accessed | tf_op | source)
XLA Modules:
  0.0 126.4 jit_solution(13696399848630493671)
XLA Ops:
  1.3 123.5 %shard_map.128 = (bf16[256,128]{1,0:T(8,128)(2,1)S(1)}, bf16[256,128]{1,0:T(8,128)(2,1)S(1)}, bf16[256,128]{1,0:T(8,128)(2,1)S(1)}, bf16[1,2048,256]{2,1,0:T(8,128)(2,1)S(1)}, bf16[1,256,2048]{2,1,0:T(8,128)(2,1)S(1)}) custom-call(bf16[256,128]{1,0:T(8,128)(2,1)} %refs_0_.1, bf16[256,128]{1,0:T(8,128)(2,1)} %refs_1_.1, bf16[256,128]{1,0:T(8,128)(2,1)} %refs_2_.1, ...), custom_call_target="tpu_custom_call" | custom-call | tf_op jit(solution)/shard_map/pallas_call | solution.py:749
  124.8 1.4 %shard_map.129 = (bf16[256,128]{1,0:T(8,128)(2,1)}, bf16[256,128]{1,0:T(8,128)(2,1)}, bf16[256,128]{1,0:T(8,128)(2,1)}, bf16[1,2048,256]{2,1,0:T(8,128)(2,1)}, bf16[1,256,2048]{2,1,0:T(8,128)(2,1)}) custom-call(bf16[256,128]{1,0:T(8,128)(2,1)S(1)} %get-tuple-element.10.refs_0_, bf16[256,128]{1,0:T(8,128)(2,1)S(1)} %get-tuple-element.11.refs_1_, ...), custom_call_target="tpu_custom_call" | custom-call | tf_op jit(solution)/shard_map/pallas_call | solution.py:769
